TPU v7x, 512 devices: a whole 4x8x8 slice. The times are simulated.
512 devices in a mesh: space: 128 (over z, y, core), fsdp: 4 (over x).
Axes of the slice: x: 4, y: 8, z: 8, core: 2. Of those that a mesh axis runs over, the one named last changes fastest.
Arguments:
- features: bfloat16 [65536, 256], P(('space', 'fsdp')), may hold values from -6 to 6
- cotangent: bfloat16 [65536, 128], P(('space', 'fsdp')), may hold values from -6 to 6
- weight: bfloat16 [256, 27, 128], P('fsdp'), may hold values from -0.078125 to 0.078125
- neighbour_map: int32 [27, 65536], P(None, ('space', 'fsdp')), may hold values from 0 to 416, as said below
- send_rows: int32 [16384], P(('space', 'fsdp')), may hold values from 0 to 128, as said below
Outputs:
- conv_out: bfloat16 [65536, 128], P(('space', 'fsdp'))
- grad_features: bfloat16 [65536, 256], P(('space', 'fsdp'))
- grad_weight: float32 [256, 27, 128], P('fsdp')
Inputs may be any that keep to these rules, and one draw needn't show every extreme that they name: `send_rows`: each block's 32 entries name local rows 0 to 127 in its live slots, which come first, and 128 in the empty slots after them; a block has at least a third of 32 live slots, rounded up, and some block has all 32 live. `neighbour_map`: entry [k, v] is a row of the table of v's block: below 128 a local row, then the 32 slots of each of the 3 x 3 neighbouring lists, and 416 for no neighbour. Offset 27 // 2 names v's own row. No entry points at slots 128 + 4 * 32 to 287.
All inputs are finite; a program needn't handle non-finite values.
Results may differ from a plain program's by a relative error of at most 0.001.
Values may be sent and summed in bfloat16 or wider, within the bound.
A program may use at most 64 MiB of HBM per device.

v0:
```python
import math

import jax
import jax.numpy as jnp
from jax import lax
from jax.sharding import PartitionSpec as P


def extended(array, sides, width):
    for axis, dim in sides:
        peers, length = (lax.axis_size(axis), array.shape[dim])
        up = [(i, (i + 1) % peers) for i in range(peers - 1)]
        down = [(j, i) for i, j in up]
        last = lax.slice_in_dim(array, length - width, length, axis=dim)
        leading = lax.slice_in_dim(array, 0, width, axis=dim)
        before = lax.ppermute(last, axis, up)
        after = lax.ppermute(leading, axis, down)
        array = jnp.concatenate([before, array, after], axis=dim)
    return array


def from_behind(array, axis, by):
    peers = lax.axis_size(axis)
    pairs = [(i, i + by) for i in range(peers) if 0 <= i + by < peers]
    return lax.ppermute(array, axis, pairs)


def body(features, cotangent, weight, neighbour_map, send_rows):
    voxels, width_in = features.shape
    width_out = cotangent.shape[1]
    offsets = neighbour_map.shape[0]
    slot_count = send_rows.shape[0]
    zero_row = jnp.zeros((1, width_in), features.dtype)
    boundary = jnp.take(jnp.concatenate([features, zero_row], 0), send_rows, axis=0)
    beside_all = extended(boundary[None, None], (("space", 0), ("fsdp", 1)), 1)
    table = jnp.concatenate([features, beside_all.reshape(9 * slot_count, width_in), zero_row], 0)
    full_weight = lax.all_gather(weight, "fsdp", axis=0, tiled=True)

    def add_offset(offset, running):
        picked = jnp.take(table, neighbour_map[offset], axis=0)
        kernel = lax.dynamic_index_in_dim(full_weight, offset, 1, keepdims=False)
        return running + jnp.dot(picked, kernel, preferred_element_type=jnp.float32)

    conv_acc = lax.fori_loop(0, offsets, add_offset, jnp.zeros((voxels, width_out), jnp.float32))
    conv_out = conv_acc.astype(jnp.bfloat16)

    def spread_offset(offset, table_grads):
        kernel = lax.dynamic_index_in_dim(full_weight, offset, 1, keepdims=False)
        term_rows = jnp.einsum("vo,io->vi", cotangent, kernel, preferred_element_type=jnp.float32)
        return table_grads.at[neighbour_map[offset]].add(term_rows)

    table_grad = lax.fori_loop(
        0, offsets, spread_offset, jnp.zeros((table.shape[0], width_in), jnp.float32)
    )
    halo_part = table_grad[voxels : voxels + 9 * slot_count].reshape(3, 3, slot_count, width_in)
    across = halo_part[1]
    for half_index, shift_by in ((0, -1), (2, 1)):
        across = across + from_behind(halo_part[half_index], "space", shift_by)
    incoming = across[1]
    for half_index, shift_by in ((0, -1), (2, 1)):
        incoming = incoming + from_behind(across[half_index], "fsdp", shift_by)
    owned_grad = jnp.concatenate([table_grad[:voxels], jnp.zeros((1, width_in), jnp.float32)], 0)
    owned_grad = owned_grad.at[send_rows].add(incoming)
    grad_features = owned_grad[:voxels].astype(jnp.bfloat16)
    total_rows = lax.axis_size("space") * lax.axis_size("fsdp") * voxels
    grad_scale = 1.0 / math.sqrt(total_rows)

    def one_offset(index_row):
        picked = jnp.take(table, index_row, axis=0)
        return jnp.einsum("vi,vo->io", picked, cotangent, preferred_element_type=jnp.float32)

    per_offset = lax.map(one_offset, neighbour_map)
    summed = lax.psum(jnp.transpose(per_offset, (1, 0, 2)) * grad_scale, "space")
    grad_weight = lax.psum_scatter(summed, "fsdp", scatter_dimension=0, tiled=True)
    return (conv_out, grad_features, grad_weight)


def solution(mesh):
    placed = (
        P(("space", "fsdp"), None),
        P(("space", "fsdp"), None),
        P("fsdp", None, None),
        P(None, ("space", "fsdp")),
        P(("space", "fsdp")),
    )
    return jax.shard_map(
        body,
        mesh=mesh,
        in_specs=placed,
        out_specs=(P(("space", "fsdp"), None), P(("space", "fsdp"), None), P("fsdp", None, None)),
        check_vma=False,
    )
```

profile of v0, /device:TPU:1, one launch (start us, length us, event | category | flops | bytes accessed | tf_op | source)
XLA Modules:
  0.0 498.3 jit_solution(11615415938224216831)
XLA Ops:
  10.1 8.7 %collective-permute-start.1 = (bf16[1,1,32,256]{3,2,1,0:T(8,128)(2,1)S(1)}, bf16[1,1,32,256]{3,2,1,0:T(8,128)(2,1)S(1)}, u32[]{:S(2)}, u32[]{:S(2)}) collective-permute-start(bf16[1,1,32,256]{3,2,1,0:T(8,128)(2,1)S(1)} %bitcast_select_fusion), channel_id=1, source_target_pairs={{4,0},{8,4},{12,8},{16,12},{20,16},{24,20},{28,24},{32,28},{36,32}... | collective-permute-start | bytes 49160 | tf_op jit(solution)/shard_map/ppermute | solution.py:17
  18.8 1.9 collective-permute-start
  23.2 4.0 collective-permute-start.2
  29.4 87.6 %while.38 = (s32[]{:T(128)}, f32[27,256,128]{2,1,0:T(8,128)}, s32[27,128]{1,0:T(8,128)}, bf16[417,256]{1,0:T(8,128)(2,1)S(1)}, bf16[128,128]{1,0:T(8,128)(2,1)}, /*index=5*/s32[]{:T(128)}) while((s32[]{:T(128)}, f32[27,256,128]{2,1,0:T(8,128)}, s32[27,128]{1,0:T(8,128)}, bf16[417,256]{1,0:T(8,128)(2,1)S(1)}, bf16[128,128]{1,0:T(8,128)(2,1)}, ...), condition=%wide.region_7.9_spmd, body=%wide.region_6.8_spmd.sunk | while | flops 8423170 | bytes 366933 | solution.py:72
  30.9 1.7 fusion.36
  34.2 1.7 fusion.36
  37.4 1.7 fusion.36
  40.7 1.7 fusion.36
  43.9 1.7 fusion.36
  47.1 1.7 fusion.36
  50.4 1.7 fusion.36
  53.6 1.7 fusion.36
  56.9 1.7 fusion.36
  60.1 1.7 fusion.36
  63.4 1.7 fusion.36
  66.6 1.7 fusion.36
  69.9 1.7 fusion.36
  73.1 1.7 fusion.36
  76.4 1.7 fusion.36
  79.6 1.7 fusion.36
  82.9 1.7 fusion.36
  86.1 1.7 fusion.36
  89.4 1.7 fusion.36
  92.6 1.7 fusion.36
  95.9 1.7 fusion.36
  99.1 1.7 fusion.36
  102.4 1.7 fusion.36
  105.6 1.7 fusion.36
  108.8 1.7 fusion.36
  112.1 1.7 fusion.36
  115.3 1.7 fusion.36
  117.0 4.1 multiply_bitcast_fusion
  121.9 87.3 %while.37 = (s32[]{:T(128)}, f32[417,256]{1,0:T(8,128)S(1)}, s32[27,128]{1,0:T(8,128)}, bf16[256,27,128]{2,0,1:T(8,128)(2,1)}, bf16[128,128]{1,0:T(8,128)(2,1)S(1)}, /*index=5*/s32[]{:T(128)}) while((s32[]{:T(128)}, f32[417,256]{1,0:T(8,128)S(1)}, s32[27,128]{1,0:T(8,128)}, bf16[256,27,128]{2,0,1:T(8,128)(2,1)}, ...), condition=%wide.region_4.6_spmd, body=%wide.region_2.0_spmd.sunk | while | flops 8421762 | bytes 886357 | solution.py:52
  123.7 1.4 scatter_fusion
  126.9 1.4 scatter_fusion
  130.2 1.4 scatter_fusion
  133.4 1.4 scatter_fusion
  136.6 1.4 scatter_fusion
  139.9 1.4 scatter_fusion
  143.1 1.4 scatter_fusion
  146.4 1.4 scatter_fusion
  149.6 1.4 scatter_fusion
  152.8 1.4 scatter_fusion
  156.1 1.4 scatter_fusion
  159.3 1.4 scatter_fusion
  162.5 1.4 scatter_fusion
  165.8 1.4 scatter_fusion
  169.0 1.4 scatter_fusion
  172.2 1.4 scatter_fusion
  175.5 1.4 scatter_fusion
  178.7 1.4 scatter_fusion
  181.9 1.4 scatter_fusion
  185.2 1.4 scatter_fusion
  188.4 1.4 scatter_fusion
  191.6 1.4 scatter_fusion
  194.9 1.4 scatter_fusion
  198.1 1.4 scatter_fusion
  201.3 1.4 scatter_fusion
  209.3 5.0 %collective-permute-start.5 = (f32[3,32,256]{2,1,0:T(8,128)S(1)}, f32[3,32,256]{2,1,0:T(8,128)S(1)}, u32[]{:S(2)}, u32[]{:S(2)}) collective-permute-start(f32[3,32,256]{2,1,0:T(8,128)S(1)} %bitcast.63), channel_id=1, source_target_pairs={{0,4},{4,8},{8,12},{12,16},{16,20},{20,24},{24,28},{28,32},{32,36}... | collective-permute-start | bytes 294920 | tf_op jit(solution)/shard_map/ppermute | solution.py:25
  214.3 1.9 collective-permute-start.4
  216.2 71.8 %while.39 = (s32[]{:T(128)}, f32[128,128]{1,0:T(8,128)S(1)}, s32[27,128]{1,0:T(8,128)}, bf16[417,256]{1,0:T(8,128)(2,1)S(1)}, bf16[256,27,128]{2,0,1:T(8,128)(2,1)}, /*index=5*/s32[]{:T(128)}, s32[]{:T(128)}) while((s32[]{:T(128)}, f32[128,128]{1,0:T(8,128)S(1)}, s32[27,128]{1,0:T(8,128)}, bf16[417,256]{1,0:T(8,128)(2,1)S(1)}, ...), condition=%wide.region_1.3_spmd.clone, body=%wide.region_0.0_spmd.clone.sunk | while | flops 8455939 | bytes 399719 | solution.py:44
  289.4 4.6 collective-permute-start.7
  296.5 193.2 %all-reduce.3.cloned.1.call-done = f32[64,27,128]{2,0,1:T(8,128)} async-done(((f32[64,27,128]{2,0,1:T(8,128)}), f32[64,27,128]{2,0,1:T(8,128)}) %all-reduce.3.cloned.1.call-update) | async-done | bytes 884752 | tf_op jit(solution)/shard_map/psum | solution.py:73
  489.6 2.2 copy.35
  (314 shorter events, 175.9 us)
Async XLA Ops:
  7.2 114.1 %all-gather.2.cloned.1.call-start = ((), (), s32[]{:S(2)}) async-start(), calls=%async_computation.1 | async-start | bytes 2211840 | tf_op jit(solution)/shard_map/all_gather | solution.py:37
  10.1 10.7 %collective-permute-start.1 = (bf16[1,1,32,256]{3,2,1,0:T(8,128)(2,1)S(1)}, bf16[1,1,32,256]{3,2,1,0:T(8,128)(2,1)S(1)}, u32[]{:S(2)}, u32[]{:S(2)}) collective-permute-start(bf16[1,1,32,256]{3,2,1,0:T(8,128)(2,1)S(1)} %bitcast_select_fusion), channel_id=1, source_target_pairs={{4,0},{8,4},{12,8},{16,12},{20,16},{24,20},{28,24},{32,28},{36,32}... | collective-permute-start | bytes 49160 | tf_op jit(solution)/shard_map/ppermute | solution.py:17
  18.8 3.1 collective-permute-start
  21.9 5.5 %collective-permute-start.3 = (bf16[3,1,32,256]{3,2,1,0:T(8,128)(2,1)S(1)}, bf16[3,1,32,256]{3,2,1,0:T(8,128)(2,1)S(1)}, u32[]{:S(2)}, u32[]{:S(2)}) collective-permute-start(bf16[3,1,32,256]{3,2,1,0:T(8,128)(2,1)S(1)} %pad_maximum_fusion.1), channel_id=1, source_target_pairs={{1,0},{2,1},{3,2},{5,4},{6,5},{7,6},{9,8},{10,9},{11,10},{13,12},{... | collective-permute-start | bytes 147464 | tf_op jit(solution)/shard_map/ppermute | solution.py:17
  23.2 5.2 %collective-permute-start.2 = (bf16[3,1,32,256]{3,2,1,0:T(8,128)(2,1)S(1)}, bf16[3,1,32,256]{3,2,1,0:T(8,128)(2,1)S(1)}, u32[]{:S(2)}, u32[]{:S(2)}) collective-permute-start(bf16[3,1,32,256]{3,2,1,0:T(8,128)(2,1)S(1)} %pad_maximum_fusion.1), channel_id=1, source_target_pairs={{0,1},{1,2},{2,3},{4,5},{5,6},{6,7},{8,9},{9,10},{10,11},{12,13},{... | collective-permute-start | bytes 147464 | tf_op jit(solution)/shard_map/ppermute | solution.py:16
  27.2 260.8 %reduce-scatter.2.cloned.1.call-start = ((), (), s32[]{:S(2)}) async-start(), calls=%async_computation.2 | async-start | bytes 4423680 | tf_op jit(solution)/shard_map/reduce_scatter | solution.py:74
  121.1 0.8 copy-start
  121.2 368.4 %all-reduce.3.cloned.1.call-start = ((), (), s32[]{:S(2)}) async-start(), calls=%async_computation.3 | async-start | bytes 1769472 | tf_op jit(solution)/shard_map/psum | solution.py:73
  209.2 84.8 %copy-start.1 = (pred[129]{0:T(512)(128)(4,1)S(1)}, pred[129]{0:T(512)(128)(4,1)}, u32[]{:S(2)}) copy-start(pred[129]{0:T(512)(128)(4,1)} %constant.104.clone.1) | copy-start | bytes 391
  209.3 78.7 %collective-permute-start.5 = (f32[3,32,256]{2,1,0:T(8,128)S(1)}, f32[3,32,256]{2,1,0:T(8,128)S(1)}, u32[]{:S(2)}, u32[]{:S(2)}) collective-permute-start(f32[3,32,256]{2,1,0:T(8,128)S(1)} %bitcast.63), channel_id=1, source_target_pairs={{0,4},{4,8},{8,12},{12,16},{16,20},{20,24},{24,28},{28,32},{32,36}... | collective-permute-start | bytes 294920 | tf_op jit(solution)/shard_map/ppermute | solution.py:25
  214.3 73.7 %collective-permute-start.4 = (f32[3,32,256]{2,1,0:T(8,128)S(1)}, f32[3,32,256]{2,1,0:T(8,128)S(1)}, u32[]{:S(2)}, u32[]{:S(2)}) collective-permute-start(f32[3,32,256]{2,1,0:T(8,128)S(1)} %bitcast.62), channel_id=1, source_target_pairs={{4,0},{8,4},{12,8},{16,12},{20,16},{24,20},{28,24},{32,28},{36,32}... | collective-permute-start | bytes 294920 | tf_op jit(solution)/shard_map/ppermute | solution.py:25
  288.1 6.6 %collective-permute-start.6 = (f32[32,256]{1,0:T(8,128)S(1)}, f32[32,256]{1,0:T(8,128)S(1)}, u32[]{:S(2)}, u32[]{:S(2)}) collective-permute-start(f32[32,256]{1,0:T(8,128)S(1)} %get-tuple-element.277), channel_id=1, source_target_pairs={{1,0},{2,1},{3,2},{5,4},{6,5},{7,6},{9,8},{10,9},{11,10},{13,12},{... | collective-permute-start | bytes 98312 | tf_op jit(solution)/shard_map/ppermute | solution.py:25
  289.4 5.6 %collective-permute-start.7 = (f32[32,256]{1,0:T(8,128)S(1)}, f32[32,256]{1,0:T(8,128)S(1)}, u32[]{:S(2)}, u32[]{:S(2)}) collective-permute-start(f32[32,256]{1,0:T(8,128)S(1)} %get-tuple-element.278), channel_id=1, source_target_pairs={{0,1},{1,2},{2,3},{4,5},{5,6},{6,7},{8,9},{9,10},{10,11},{12,13},{... | collective-permute-start | bytes 98312 | tf_op jit(solution)/shard_map/ppermute | solution.py:25
Sparse Core Ops, SparseCore 0:
  27.4 35.6 all-gather.1
  121.3 50.5 reduce-scatter.1
  288.2 201.3 all-reduce.2
where the time goes:
time: 506 us; the launch traced here: 498 us
  waiting for transfers between devices  196 us (39%)
  other arithmetic  103 us (20%)
  matrix products  101 us (20%)
  local copies, waits for them, and re-layouts  53.5 us (11%)
  starting transfers between devices  28.9 us (6%)
  between operations  14 us (3%)
    psum x1, waiting for transfers between devices, body(): lax.psum(jnp.transpose(per_offset, (1, 0, 2)) * grad_scale, 'space')  193 us
    dot_general x27, matrix products, one_offset(): jnp.einsum('vi,vo->io', picked, cotangent, preferred_element_type=jnp.flo...  45.7 us
    scatter-add x27, other arithmetic, spread_offset(): return table_grads.at[neighbour_map[offset]].add(term_rows)  38 us
    dot_general x27, matrix products, add_offset(): return running + jnp.dot(picked, kernel, preferred_element_type=jnp.float32)  29 us
    dot_general x27, matrix products, spread_offset(): jnp.einsum('vo,io->vi', cotangent, kernel, preferred_element_type=jnp.flo...  26.8 us
    gather x27, local copies, waits for them, and re-layouts, one_offset(): picked = jnp.take(table, index_row, axis=0)  22.9 us
    gather x27, local copies, waits for them, and re-layouts, add_offset(): picked = jnp.take(table, neighbour_map[offset], axis=0)  22.9 us
    and x27, other arithmetic, add_offset(): picked = jnp.take(table, neighbour_map[offset], axis=0)  18.9 us
  transfers between devices with their start and end apart: 11, of which 4 were waited for; matrix products, arithmetic and copies ran while one was open for 51% of the time, Pallas kernels for 0%

commit v1 on v0

v1 whole, which is shorter than its diff:
```python
import math

import jax
import jax.numpy as jnp
from jax import lax
from jax.experimental import pallas as pl
from jax.experimental.pallas import tpu as pltpu
from jax.sharding import PartitionSpec as P

MESH = pl.DeviceIdType.MESH
VMEM = pl.BlockSpec(memory_space=pltpu.VMEM)
SIDES = [(a, c) for a in range(3) for c in range(3) if (a, c) != (1, 1)]
NS, NF, NY, NZ = 128, 4, 8, 8
VOX, HC, CI, CO, KV, KP = 128, 32, 256, 128, 27, 28
IL = CI // NF
ROWS = KP * IL
HALF = ROWS // 2
PART = HALF // NY
TAB = VOX + 8 * HC
FSDP_ORDER = (2, 1, 3)


def position():
    s, f = lax.axis_index("space"), lax.axis_index("fsdp")
    core = lax.rem(s, 2)
    y = lax.rem(s // 2, NY)
    z = s // (2 * NY)
    return s, f, core, y, z


def shifted(s, f, ds, df):
    return (lax.rem(s + ds + NS, NS), lax.rem(f + df + NF, NF))


def meet(targets):
    barrier = pltpu.get_barrier_semaphore()
    for target in targets:
        pl.semaphore_signal(barrier, inc=1, device_id=target, device_id_type=MESH)
    pl.semaphore_wait(barrier, len(targets))


def remote(src, dst, send, recv, target):
    return pltpu.make_async_remote_copy(
        src_ref=src, dst_ref=dst, send_sem=send, recv_sem=recv, device_id=target, device_id_type=MESH
    )


def spread_kernel(b_ref, w_ref, beside_ref, wall_ref, hs, hr, xs, xr, ps, pr, own_sem):
    s, f, core, y, z = position()
    partner = (s + 1 - 2 * core, f)
    meet([shifted(s, f, 1 - a, 1 - c) for a, c in SIDES] + [shifted(s, f, 0, 2)] + [partner])
    copies = []
    for n, (a, c) in enumerate(SIDES):
        copies.append(remote(b_ref, beside_ref.at[n], hs.at[n], hr.at[n], shifted(s, f, 1 - a, 1 - c)))
        copies[-1].start()
    own = pltpu.make_async_copy(w_ref, wall_ref.at[f], own_sem)
    own.start()
    across = {}
    for d in FSDP_ORDER:
        target = shifted(s, f, 0, d)
        across[d] = remote(w_ref.at[core], wall_ref.at[f, core], xs.at[d], xr.at[d], target)
        across[d].start()
    handed = []
    for d in (1, 3, 2):
        source = lax.rem(f - d + NF, NF)
        got = wall_ref.at[source, core]
        remote(got, got, xs.at[d], xr.at[d], partner).wait_recv()
        handed.append((d, remote(got, got, ps.at[d], pr.at[d], partner)))
        handed[-1][1].start()
    for d, copy in handed:
        source = lax.rem(f - d + NF, NF)
        there = wall_ref.at[source, 1 - core]
        remote(there, there, ps.at[d], pr.at[d], partner).wait_recv()
        copy.wait_send()
    for d in FSDP_ORDER:
        across[d].wait_send()
    own.wait()
    for copy in copies:
        copy.wait()


def compute_kernel(feat_ref, beside_ref, map_ref, mapt_ref, cot_ref, w_ref, conv_ref, gw_ref, own_ref, halo_ref, tab, tg):
    tab[:VOX, :] = feat_ref[...]
    tab[VOX:, :] = beside_ref[...].reshape(8 * HC, CI)
    cot = cot_ref[...]
    lanes = lax.broadcasted_iota(jnp.int32, (VOX, TAB), 1)
    rows = lax.broadcasted_iota(jnp.int32, (TAB, VOX), 0)
    acc = jnp.zeros((VOX, CO), jnp.float32)
    scale = 1.0 / math.sqrt(NS * NF * VOX)
    group = 3
    for g in range(KV // group):
        hot, high, low = [], [], []
        for k in range(g * group, (g + 1) * group):
            col = mapt_ref[:, k : k + 1]
            pick = (lanes == col).astype(jnp.bfloat16)
            picked = jnp.dot(pick, tab[...], preferred_element_type=jnp.float32).astype(jnp.bfloat16)
            kernel = w_ref[:, k].reshape(CI, CO)
            acc = acc + jnp.dot(picked, kernel, preferred_element_type=jnp.float32)
            gw = lax.dot_general(picked, cot, (((0,), (0,)), ((), ())), preferred_element_type=jnp.float32) * scale
            for q in range(NF):
                gw_ref[q, k * IL : (k + 1) * IL, :] = gw[q * IL : (q + 1) * IL]
            term = lax.dot_general(cot, kernel, (((1,), (1,)), ((), ())), preferred_element_type=jnp.float32)
            top = term.astype(jnp.bfloat16)
            high.append(top)
            low.append((term - top.astype(jnp.float32)).astype(jnp.bfloat16))
            hot.append((rows == map_ref[k : k + 1, :]).astype(jnp.bfloat16))
        hot_all = jnp.concatenate(hot, 1)
        both = jnp.concatenate([jnp.concatenate(high, 0), jnp.concatenate(low, 0)], 1)
        new = jnp.dot(hot_all, both, preferred_element_type=jnp.float32)
        if g == 0:
            tg[...] = new
        else:
            tg[...] += new
    gw_ref[:, KV * IL :, :] = jnp.zeros((NF, IL, CO), jnp.float32)
    conv_ref[...] = acc.astype(jnp.bfloat16)
    own_ref[...] = tg[:VOX, :CI] + tg[:VOX, CI:]
    halo_ref[...] = (tg[VOX:, :CI] + tg[VOX:, CI:]).reshape(8, HC, CI)


def reduce_kernel(gw_ref, halo_ref, total_ref, back_ref, pbuf, acc0, xbuf, acc1, ybuf, acc2, zbuf,
                  hs, hr, ps, pr, xs, xr, ys, yr, zs, zr, gs, gr, cs, cr):
    s, f, core, y, z = position()
    other = 1 - core
    partner = (s + 1 - 2 * core, f)

    def y_peer(d):
        return ((z * NY + lax.rem(y + d, NY)) * 2 + core, f)

    def z_peer(d):
        return ((lax.rem(z + d, NZ) * NY + y) * 2 + core, f)

    meet(
        [shifted(s, f, a - 1, c - 1) for a, c in SIDES]
        + [partner]
        + [shifted(s, f, 0, 2)]
        + [y_peer(d) for d in range(1, NY)]
        + [z_peer(d) for d in range(1, NZ)]
    )
    order = (2, 1, 3, 0)
    pairs = {}
    for d in order:
        j = lax.rem(f + d, NF)
        src = gw_ref.at[j, pl.ds(other * HALF, HALF), :]
        pairs[d] = remote(src, pbuf.at[d], ps.at[d], pr.at[d], partner)
        pairs[d].start()
    copies = []
    for n, (a, c) in enumerate(SIDES):
        copies.append(remote(halo_ref.at[n], back_ref.at[n], hs.at[n], hr.at[n], shifted(s, f, a - 1, c - 1)))
        copies[-1].start()
    across = {}
    for d in order:
        j = lax.rem(f + d, NF)
        pairs[d].wait_recv()

        def add_pair(i, _):
            here = pl.ds(pl.multiple_of(i * PART, 8), PART)
            mine = pl.ds(pl.multiple_of(core * HALF + i * PART, 8), PART)
            acc0[d, here, :] = gw_ref[j, mine, :] + pbuf[d, here, :]
            return 0

        lax.fori_loop(0, NY, add_pair, 0)
        if d != 0:
            across[d] = remote(acc0.at[d], xbuf.at[d - 1], xs.at[d], xr.at[d], shifted(s, f, 0, d))
            across[d].start()
    for d in FSDP_ORDER:
        across[d].wait_recv()

    def add_x(i, _):
        here = pl.ds(pl.multiple_of(i * PART, 8), PART)
        acc1[i] = (acc0[0, here, :] + xbuf[0, here, :]) + (xbuf[1, here, :] + xbuf[2, here, :])
        return 0

    lax.fori_loop(0, NY, add_x, 0)
    y_copies = []
    for d in range(1, NY):
        y_copies.append(remote(acc1.at[lax.rem(y + d, NY)], ybuf.at[d], ys.at[d], yr.at[d], y_peer(d)))
        y_copies[-1].start()
    for copy in y_copies:
        copy.wait_recv()
    running = acc1[y]
    for d in range(1, NY):
        running = running + ybuf[d]
    acc2[...] = running
    zbuf[z] = running
    z_copies = []
    for d in range(1, NZ):
        z_copies.append(remote(acc2, zbuf.at[z], zs.at[d], zr.at[d], z_peer(d)))
        z_copies[-1].start()
    for d in range(1, NZ):
        from_z = zbuf.at[lax.rem(z - d + NZ, NZ)]
        remote(from_z, from_z, zs.at[d], zr.at[d], partner).wait_recv()
    done = zbuf[0]
    for q in range(1, NZ):
        done = done + zbuf[q]

    def spot(side, at):
        return total_ref.at[side * NY + at]

    total_ref[core * NY + y] = done
    mine = spot(core, y)
    g_copies = []
    for d in range(1, NY):
        g_copies.append(remote(mine, mine, gs.at[d], gr.at[d], y_peer(d)))
        g_copies[-1].start()
    handed = [remote(mine, mine, cs.at[0], cr.at[0], partner)]
    handed[0].start()
    for d in range(1, NY):
        got = spot(core, lax.rem(y - d + NY, NY))
        remote(got, got, gs.at[d], gr.at[d], partner).wait_recv()
        handed.append(remote(got, got, cs.at[d], cr.at[d], partner))
        handed[-1].start()
    for d in range(NY):
        there = spot(other, lax.rem(y - d + NY, NY))
        remote(there, there, cs.at[d], cr.at[d], partner).wait_recv()
        handed[d].wait_send()
    for copy in copies:
        copy.wait()
    for d in order:
        pairs[d].wait_send()
    for d in FSDP_ORDER:
        across[d].wait_send()
    for copy in y_copies + z_copies + g_copies:
        copy.wait_send()


def dma(n):
    return pltpu.SemaphoreType.DMA((n,))


def body(features, cotangent, weight, neighbour_map, send_rows):
    f32, bf16 = jnp.float32, jnp.bfloat16
    pick = (send_rows[:, None] == jnp.arange(VOX)[None, :]).astype(bf16)
    boundary = jnp.dot(pick, features, preferred_element_type=f32).astype(bf16)
    by_offset = jnp.pad(jnp.transpose(weight, (1, 0, 2)), ((0, 1), (0, 0), (0, 0)))
    beside, wall = pl.pallas_call(
        spread_kernel,
        out_shape=(
            jax.ShapeDtypeStruct((8, HC, CI), bf16),
            jax.ShapeDtypeStruct((NF, 2, KP // 2, IL, CO), bf16),
        ),
        in_specs=[VMEM] * 2,
        out_specs=(VMEM, VMEM),
        scratch_shapes=[dma(8), dma(8), dma(NF), dma(NF), dma(NF), dma(NF), pltpu.SemaphoreType.DMA],
        compiler_params=pltpu.CompilerParams(collective_id=0, has_side_effects=True),
        name="spread",
    )(boundary, by_offset.reshape(2, KP // 2, IL, CO))
    s, f = lax.axis_index("space"), lax.axis_index("fsdp")

    def inside(sign):
        ok = [
            (s + sign * (a - 1) >= 0) & (s + sign * (a - 1) < NS) & (f + sign * (c - 1) >= 0) & (f + sign * (c - 1) < NF)
            for a, c in SIDES
        ]
        return jnp.stack(ok)[:, None, None]

    beside = jnp.where(inside(1), beside, jnp.zeros_like(beside))
    spots = jnp.where(neighbour_map >= VOX + 5 * HC, neighbour_map - HC, neighbour_map)
    conv_out, gw, own, halo = pl.pallas_call(
        compute_kernel,
        out_shape=(
            jax.ShapeDtypeStruct((VOX, CO), bf16),
            jax.ShapeDtypeStruct((NF, ROWS, CO), f32),
            jax.ShapeDtypeStruct((VOX, CI), f32),
            jax.ShapeDtypeStruct((8, HC, CI), f32),
        ),
        in_specs=[VMEM] * 6,
        out_specs=(VMEM,) * 4,
        scratch_shapes=[pltpu.VMEM((TAB, CI), bf16), pltpu.VMEM((TAB, 2 * CI), f32)],
        compiler_params=pltpu.CompilerParams(vmem_limit_bytes=40 << 20),
        name="stencil",
    )(features, beside, spots, spots.T, cotangent, wall.reshape(NF, KP, IL, CO))
    total, back = pl.pallas_call(
        reduce_kernel,
        out_shape=(
            jax.ShapeDtypeStruct((2 * NY, PART, CO), f32),
            jax.ShapeDtypeStruct((8, HC, CI), f32),
        ),
        in_specs=[VMEM] * 2,
        out_specs=(VMEM, VMEM),
        scratch_shapes=[
            pltpu.VMEM((NF, HALF, CO), f32),
            pltpu.VMEM((NF, HALF, CO), f32),
            pltpu.VMEM((NF - 1, HALF, CO), f32),
            pltpu.VMEM((NY, PART, CO), f32),
            pltpu.VMEM((NY, PART, CO), f32),
            pltpu.VMEM((PART, CO), f32),
            pltpu.VMEM((NZ, PART, CO), f32),
        ]
        + [dma(8)] * 2 + [dma(NF)] * 4 + [dma(NY)] * 2 + [dma(NZ)] * 2 + [dma(NY)] * 4,
        compiler_params=pltpu.CompilerParams(collective_id=1, has_side_effects=True, vmem_limit_bytes=40 << 20),
        name="reduce",
    )(gw, halo)
    incoming = jnp.sum(jnp.where(inside(-1), back, 0.0), 0)
    put = (jnp.arange(VOX)[:, None] == send_rows[None, :]).astype(f32)
    settled = own + jnp.dot(put, incoming, preferred_element_type=f32, precision=lax.Precision.HIGHEST)
    grad_weight = jnp.transpose(total.reshape(KP, IL, CO)[:KV], (1, 0, 2))
    return (conv_out, settled.astype(bf16), grad_weight)


def solution(mesh):
    rows = P(("space", "fsdp"), None)
    placed = (rows, rows, P("fsdp", None, None), P(None, ("space", "fsdp")), P(("space", "fsdp")))
    return jax.shard_map(
        body, mesh=mesh, in_specs=placed, out_specs=(rows, rows, P("fsdp", None, None)), check_vma=False
    )
```

time: 506 us -> 118 us (0.23); the launches traced: 498 us -> 118 us
  waiting for transfers between devices: 196 us -> 0 us
  Pallas kernels: 0 us -> 106 us
  other arithmetic: 103 us -> 1.08 us
  matrix products: 101 us -> 2.48 us
  local copies, waits for them, and re-layouts: 53.5 us -> 7.04 us
  starting transfers between devices: 28.9 us -> 0 us
  between operations: 14 us -> 0.72 us
    psum x1 -> x0, waiting for transfers between devices: 193 us -> none  [body(): lax.psum(jnp.transpose(per_offset, (1, 0, 2)) * grad_scale, 'space')]
    pallas_call x0 -> x3, Pallas kernels: none -> 106 us  [the longest x1 70.2 us: body(): pl.pallas_call(reduce_kernel, out_shape=(jax.ShapeDtypeStruct((2 * NY, PA...]
    dot_general x81 -> x2, matrix products: 101 us -> 2.48 us  [the longest x1 1.66 us: body(): boundary = jnp.dot(pick, features, preferred_element_type=f32).astype(bf16)]
    gather x55 -> x0, local copies, waits for them, and re-layouts: 46.4 us -> none  [the longest x27 22.9 us: one_offset(): picked = jnp.take(table, index_row, axis=0)]
    scatter-add x28 -> x0, other arithmetic: 38.8 us -> none  [the longest x27 38 us: spread_offset(): return table_grads.at[neighbour_map[offset]].add(term_rows)]
    and x55 -> x0, other arithmetic: 38.4 us -> none  [the longest x27 18.9 us: add_offset(): picked = jnp.take(table, neighbour_map[offset], axis=0)]
    ppermute x8 -> x0, starting transfers between devices: 28.8 us -> none  [the longest x4 12.8 us: from_behind(): return lax.ppermute(array, axis, pairs)]
    select_n x29 -> x1, other arithmetic: 19.6 us -> 0.99 us  [body(): beside = jnp.where(inside(1), beside, jnp.zeros_like(beside))]
  transfers between devices with their start and end apart: 11 -> 0, of which waited for: 4 -> 0; matrix products, arithmetic and copies ran while one was open for 51% -> 0% of each run, Pallas kernels for 0% -> 0%
where the time goes in v1:
time: 118 us
  Pallas kernels  106 us (90%)
  local copies, waits for them, and re-layouts  7.04 us (6%)
  matrix products  2.48 us (2%)
    pallas_call x1, Pallas kernels, body(): pl.pallas_call(reduce_kernel, out_shape=(jax.ShapeDtypeStruct((2 * NY, PA...  70.2 us
    pallas_call x1, Pallas kernels, body(): pl.pallas_call(spread_kernel, out_shape=(jax.ShapeDtypeStruct((8, HC, CI)...  28 us
    pallas_call x1, Pallas kernels, body(): pl.pallas_call(compute_kernel, out_shape=(jax.ShapeDtypeStruct((VOX, CO),...  8.2 us
    unnamed x9, local copies, waits for them, and re-layouts  3.91 us

profile of v1, /device:TPU:1, one launch (start us, length us, event | category | flops | bytes accessed | tf_op | source)
XLA Modules:
  0.0 117.8 jit_solution(17706634082778651224)
XLA Ops:
  0.7 0.1 stack.47
  0.8 0.1 stack.46
  0.9 1.7 %convolution_convert_fusion.b_ref = bf16[32,256]{1,0:T(8,128)(2,1)} fusion(bf16[128,256]{1,0:T(8,128)(2,1)} %feat_ref.1, s32[32]{0:T(128)} %param.9), kind=kOutput, calls=%fused_computation.2 | convolution fusion | flops 2109440 | bytes 82048 | tf_op jit(solution)/shard_map/dot_general | solution.py:233
  2.5 0.8 copy.8
  3.4 0.1 copy.11.map_ref
  3.4 1.8 %pad.4 = bf16[28,64,128]{2,1,0:T(8,128)(2,1)} pad(bf16[27,64,128]{2,1,0:T(8,128)(2,1)} %bitcast.21, bf16[]{:T(256)} %constant.25.clone.1), padding=0_1x0_0x0_0 | pad | bytes 901122 | tf_op jit(solution)/shard_map/jit(_pad)/pad | solution.py:234
  5.3 0.0 copy-start.3
  5.3 28.0 %spread.1 = (bf16[8,32,256]{2,1,0:T(8,128)(2,1)}, bf16[4,2,14,64,128]{4,3,2,1,0:T(8,128)(2,1)}) custom-call(bf16[32,256]{1,0:T(8,128)(2,1)} %convolution_convert_fusion.b_ref, bf16[2,14,64,128]{3,2,1,0:T(8,128)(2,1)} %bitcast.20), custom_call_target="tpu_custom_call" | custom-call | tf_op jit(solution)/shard_map/spread/pallas_call | solution.py:235
  33.3 1.0 broadcast_select_fusion.beside_ref
  34.3 0.0 copy-start
  34.3 1.5 %copy-done = bf16[4,2,14,64,128]{4,3,2,1,0:T(8,128)(2,1)S(1)} copy-done((bf16[4,2,14,64,128]{4,3,2,1,0:T(8,128)(2,1)S(1)}, bf16[4,2,14,64,128]{4,3,2,1,0:T(8,128)(2,1)}, u32[]{:S(2)}) %copy-start) | copy-done | bytes 1835032
  35.8 0.0 copy-start.1
  35.8 0.8 copy-done.1
  36.6 0.0 copy-start.2
  36.6 0.8 copy-done.2
  37.4 8.2 %stencil.1 = (bf16[128,128]{1,0:T(8,128)(2,1)}, f32[4,1792,128]{2,1,0:T(8,128)S(1)}, f32[128,256]{1,0:T(8,128)S(1)}, f32[8,32,256]{2,1,0:T(8,128)S(1)}) custom-call(bf16[128,256]{1,0:T(8,128)(2,1)S(1)} %copy-done.1, bf16[8,32,256]{2,1,0:T(8,128)(2,1)S(1)} %broadcast_select_fusion.beside_ref, s32[27,128]{1,0:T(8,128)S(1)} %copy.11.map_ref, ...), custom_call_target="tpu_custom_call" | custom-call | tf_op jit(solution)/shard_map/stencil/pallas_call | solution.py:258
  45.6 70.2 %reduce.1 = (f32[16,112,128]{2,1,0:T(8,128)S(1)}, f32[8,32,256]{2,1,0:T(8,128)S(1)}) custom-call(f32[4,1792,128]{2,1,0:T(8,128)S(1)} %get-tuple-element.15.gw_ref, f32[8,32,256]{2,1,0:T(8,128)S(1)} %get-tuple-element.16.halo_ref), custom_call_target="tpu_custom_call" | custom-call | tf_op jit(solution)/shard_map/reduce/pallas_call | solution.py:272
  115.8 0.1 select_reduce_fusion
  115.9 0.0 copy-done.3
  115.9 0.8 fusion
  116.8 1.0 slice_bitcast_fusion
  (1 shorter events, 0.0 us)
Async XLA Ops:
  5.3 110.6 %copy-start.3 = (s32[32]{0:T(128)S(1)}, s32[32]{0:T(128)}, u32[]{:S(2)}) copy-start(s32[32]{0:T(128)} %param.9) | copy-start | bytes 388
  34.3 1.5 %copy-start = (bf16[4,2,14,64,128]{4,3,2,1,0:T(8,128)(2,1)S(1)}, bf16[4,2,14,64,128]{4,3,2,1,0:T(8,128)(2,1)}, u32[]{:S(2)}) copy-start(bf16[4,2,14,64,128]{4,3,2,1,0:T(8,128)(2,1)} %get-tuple-element.12) | copy-start | bytes 5505028
  35.8 0.8 copy-start.1
  36.6 0.8 copy-start.2

commit v2 on v1

v2 whole, which is shorter than its diff:
```python
import math

import jax
import jax.numpy as jnp
from jax import lax
from jax.experimental import pallas as pl
from jax.experimental.pallas import tpu as pltpu
from jax.sharding import PartitionSpec as P

MESH = pl.DeviceIdType.MESH
VMEM = pl.BlockSpec(memory_space=pltpu.VMEM)
SIDES = [(a, c) for a in range(3) for c in range(3) if (a, c) != (1, 1)]
NS, NF, NY, NZ = 128, 4, 8, 8
VOX, HC, CI, CO, KV, KP = 128, 32, 256, 128, 27, 28
IL = CI // NF
ROWS = KP * IL
HALF = ROWS // 2
LINE = HALF // 2
SKIP = KV // 2
CHUNK = LINE // NY
PART = 112
TAB = VOX + 8 * HC


def position():
    s, f = lax.axis_index("space"), lax.axis_index("fsdp")
    core = lax.rem(s, 2)
    y = lax.rem(s // 2, NY)
    z = s // (2 * NY)
    return s, f, core, y, z


def shifted(s, f, ds, df):
    return (lax.rem(s + ds + NS, NS), lax.rem(f + df + NF, NF))


def meet(targets):
    barrier = pltpu.get_barrier_semaphore()
    for target in targets:
        pl.semaphore_signal(barrier, inc=1, device_id=target, device_id_type=MESH)
    pl.semaphore_wait(barrier, len(targets))


def remote(src, dst, send, recv, target):
    return pltpu.make_async_remote_copy(
        src_ref=src, dst_ref=dst, send_sem=send, recv_sem=recv, device_id=target, device_id_type=MESH
    )


def spread_kernel(b_ref, w_ref, beside_ref, wall_ref, hs, hr, xs, xr, ps, pr, own_sem):
    s, f, core, y, z = position()
    partner = (s + 1 - 2 * core, f)
    left, right = shifted(s, f, 0, -1), shifted(s, f, 0, 1)
    from_left, from_right, opposite = left[1], right[1], lax.rem(f + 2, NF)
    meet([shifted(s, f, 1 - a, 1 - c) for a, c in SIDES] + [partner])
    copies = []
    for n, (a, c) in enumerate(SIDES):
        copies.append(remote(b_ref, beside_ref.at[n], hs.at[n], hr.at[n], shifted(s, f, 1 - a, 1 - c)))
        copies[-1].start()
    own = [pltpu.make_async_copy(w_ref.at[pl.ds(h * SKIP, SKIP + 1)], wall_ref.at[f, h], own_sem.at[h]) for h in range(2)]
    own[0].start()
    own[1].start()
    quarter = KP // 4
    first, second = pl.ds(0, quarter), pl.ds(quarter, quarter)
    mine = w_ref.at[pl.ds(core * SKIP, SKIP + 1)]
    across = [
        remote(mine, wall_ref.at[f, core], xs.at[0], xr.at[0], right),
        remote(mine, wall_ref.at[f, core], xs.at[1], xr.at[1], left),
    ]
    across[0].start()
    across[1].start()

    def landed(side):
        return (
            wall_ref.at[from_left, side],
            wall_ref.at[from_right, side],
            wall_ref.at[opposite, side, first],
            wall_ref.at[opposite, side, second],
        )

    handed = []
    for m, got in enumerate(landed(core)):
        remote(got, got, xs.at[m], xr.at[m], partner).wait_recv()
        if m == 0:
            piece = wall_ref.at[from_left, core, first]
            across.append(remote(piece, piece, xs.at[2], xr.at[2], right))
            across[-1].start()
        if m == 1:
            piece = wall_ref.at[from_right, core, second]
            across.append(remote(piece, piece, xs.at[3], xr.at[3], left))
            across[-1].start()
        handed.append(remote(got, got, ps.at[m], pr.at[m], partner))
        handed[-1].start()
    for m, there in enumerate(landed(1 - core)):
        remote(there, there, ps.at[m], pr.at[m], partner).wait_recv()
    for copy in handed + across:
        copy.wait_send()
    own[0].wait()
    own[1].wait()
    for copy in copies:
        copy.wait()


def compute_kernel(feat_ref, beside_ref, map_ref, mapt_ref, cot_ref, w_ref, conv_ref, gw_ref, own_ref, halo_ref, tab, tg):
    tab[:VOX, :] = feat_ref[...]
    s, f, core, y, z = position()
    for n, (a, c) in enumerate(SIDES):
        outer, inner = s + a - 1, f + c - 1
        ok = (outer >= 0) & (outer < NS) & (inner >= 0) & (inner < NF)
        rows_n = beside_ref[n]
        tab[VOX + n * HC : VOX + (n + 1) * HC, :] = jnp.where(ok, rows_n, jnp.zeros_like(rows_n))
    cot = cot_ref[...]
    lanes = lax.broadcasted_iota(jnp.int32, (VOX, TAB), 1)
    rows = lax.broadcasted_iota(jnp.int32, (TAB, VOX), 0)
    acc = jnp.zeros((VOX, CO), jnp.float32)
    scale = 1.0 / math.sqrt(NS * NF * VOX)
    group = 3
    for g in range(KV // group):
        hot, high, low = [], [], []
        for k in range(g * group, (g + 1) * group):
            col = mapt_ref[:, k : k + 1]
            pick = (lanes == col).astype(jnp.bfloat16)
            picked = jnp.dot(pick, tab[...], preferred_element_type=jnp.float32).astype(jnp.bfloat16)
            kernel = w_ref[:, k // (SKIP + 1), k - k // (SKIP + 1) * SKIP].reshape(CI, CO)
            acc = acc + jnp.dot(picked, kernel, preferred_element_type=jnp.float32)
            gw = lax.dot_general(picked, cot, (((0,), (0,)), ((), ())), preferred_element_type=jnp.float32) * scale
            for q in range(NF):
                gw_ref[q, k * IL : (k + 1) * IL, :] = gw[q * IL : (q + 1) * IL]
            term = lax.dot_general(cot, kernel, (((1,), (1,)), ((), ())), preferred_element_type=jnp.float32)
            top = term.astype(jnp.bfloat16)
            high.append(top)
            low.append((term - top.astype(jnp.float32)).astype(jnp.bfloat16))
            hot.append((rows == map_ref[k : k + 1, :]).astype(jnp.bfloat16))
        hot_all = jnp.concatenate(hot, 1)
        both = jnp.concatenate([jnp.concatenate(high, 0), jnp.concatenate(low, 0)], 1)
        new = jnp.dot(hot_all, both, preferred_element_type=jnp.float32)
        if g == 0:
            tg[...] = new
        else:
            tg[...] += new
    gw_ref[:, KV * IL :, :] = jnp.zeros((NF, IL, CO), jnp.float32)
    conv_ref[...] = acc.astype(jnp.bfloat16)
    own_ref[...] = tg[:VOX, :CI] + tg[:VOX, CI:]
    halo_ref[...] = (tg[VOX:, :CI] + tg[VOX:, CI:]).reshape(8, HC, CI)


def reduce_kernel(gw_ref, halo_ref, total_ref, back_ref, pbuf, acc0, rbuf, xbuf, acc1, ubuf, acc2, vbuf,
                  hs, hr, ps, pr, xs, xr, us, ur, vs, vr, gs, gr, cs, cr):
    s, f, core, y, z = position()
    other = 1 - core
    partner = (s + 1 - 2 * core, f)
    left, right = shifted(s, f, 0, -1), shifted(s, f, 0, 1)

    def y_peer(d):
        return ((z * NY + lax.rem(y + d, NY)) * 2 + core, f)

    def z_peer(d):
        return ((lax.rem(z + d, NZ) * NY + y) * 2 + core, f)

    lines = ((y, y_peer), (z, z_peer))
    meet(
        [shifted(s, f, a - 1, c - 1) for a, c in SIDES]
        + [partner]
        + [y_peer(d) for d in range(1, NY)]
        + [z_peer(d) for d in range(1, NZ)]
    )
    order = (2, 1, 3, 0)
    pairs = {}
    for d in order:
        src = gw_ref.at[lax.rem(f + d, NF), pl.ds(other * HALF, HALF), :]
        pairs[d] = remote(src, pbuf.at[d], ps.at[d], pr.at[d], partner)
        pairs[d].start()
    copies = []
    for n, (a, c) in enumerate(SIDES):
        copies.append(remote(halo_ref.at[n], back_ref.at[n], hs.at[n], hr.at[n], shifted(s, f, a - 1, c - 1)))
        copies[-1].start()
    half_a, half_b = pl.ds(0, LINE), pl.ds(LINE, LINE)
    across = {}

    def send_x(m, src, dst, target):
        across[m] = remote(src, dst, xs.at[m], xr.at[m], target)
        across[m].start()

    for d in order:
        j = lax.rem(f + d, NF)
        pairs[d].wait_recv()

        def add_pair(i, _):
            here = pl.ds(pl.multiple_of(i * PART, 8), PART)
            mine = pl.ds(pl.multiple_of(core * HALF + i * PART, 8), PART)
            acc0[d, here, :] = gw_ref[j, mine, :] + pbuf[d, here, :]
            return 0

        lax.fori_loop(0, HALF // PART, add_pair, 0)
        if d == 2:
            send_x(0, acc0.at[2, half_a], rbuf.at[0], right)
            send_x(1, acc0.at[2, half_b], rbuf.at[1], left)
        if d == 1:
            send_x(2, acc0.at[1, half_b], xbuf.at[0, half_b], right)
        if d == 3:
            send_x(3, acc0.at[3, half_a], xbuf.at[1, half_a], left)

    for m, d, begin, half, target in ((0, 1, 0, half_a, right), (1, 3, LINE, half_b, left)):
        across[m].wait_recv()

        def add_relay(i, _):
            here = pl.ds(pl.multiple_of(begin + i * PART, 8), PART)
            acc0[d, here, :] += rbuf[m, pl.ds(pl.multiple_of(i * PART, 8), PART), :]
            return 0

        lax.fori_loop(0, LINE // PART, add_relay, 0)
        send_x(4 + m, acc0.at[d, half], xbuf.at[m, half], target)

    u_copies = []
    for t, needs in enumerate(((3, 4), (2, 5))):
        for m in needs:
            across[m].wait_recv()

        def add_x(i, _):
            here = pl.ds(pl.multiple_of(t * LINE + i * CHUNK, 8), CHUNK)
            acc1[t, i] = acc0[0, here, :] + (xbuf[0, here, :] + xbuf[1, here, :])
            return 0

        lax.fori_loop(0, NY, add_x, 0)
        at, peer = lines[t]
        for d in range(1, NY):
            u_copies.append(remote(acc1.at[t, lax.rem(at + d, NY)], ubuf.at[t, d], us.at[t, d], ur.at[t, d], peer(d)))
            u_copies[-1].start()
    v_copies = []
    for t in range(2):
        for copy in u_copies[t * 7 : t * 7 + 7]:
            copy.wait_recv()
        running = acc1[t, lines[t][0]]
        for d in range(1, NY):
            running = running + ubuf[t, d]
        acc2[t] = running
        at, peer = lines[1 - t]
        vbuf[t, at] = running
        for d in range(1, NZ):
            v_copies.append(remote(acc2.at[t], vbuf.at[t, at], vs.at[t, d], vr.at[t, d], peer(d)))
            v_copies[-1].start()
    g_copies, handed = [], []
    for t in range(2):
        across_at = lines[1 - t][0]
        for d in range(1, NZ):
            got = vbuf.at[t, lax.rem(across_at - d + NZ, NZ)]
            remote(got, got, vs.at[t, d], vr.at[t, d], partner).wait_recv()
        done = vbuf[t, 0]
        for q in range(1, NZ):
            done = done + vbuf[t, q]
        at, peer = lines[t]
        total_ref[core, t, at] = done
        mine = total_ref.at[core, t, at]
        for d in range(1, NY):
            g_copies.append(remote(mine, mine, gs.at[t, d], gr.at[t, d], peer(d)))
            g_copies[-1].start()
        handed.append(remote(mine, mine, cs.at[t, 0], cr.at[t, 0], partner))
        handed[-1].start()
    for copy in copies:
        copy.wait()
    for d in range(1, NY):
        for t in range(2):
            got = total_ref.at[core, t, lax.rem(lines[t][0] - d + NY, NY)]
            remote(got, got, gs.at[t, d], gr.at[t, d], partner).wait_recv()
            handed.append(remote(got, got, cs.at[t, d], cr.at[t, d], partner))
            handed[-1].start()
    for d in range(NY):
        for t in range(2):
            there = total_ref.at[other, t, lax.rem(lines[t][0] - d + NY, NY)]
            remote(there, there, cs.at[t, d], cr.at[t, d], partner).wait_recv()
    for copy in handed + u_copies + v_copies + g_copies:
        copy.wait_send()
    for d in order:
        pairs[d].wait_send()
    for m in range(6):
        across[m].wait_send()


def dma(n):
    return pltpu.SemaphoreType.DMA((n,))


def body(features, cotangent, weight, neighbour_map, send_rows):
    f32, bf16 = jnp.float32, jnp.bfloat16
    pick = (send_rows[:, None] == jnp.arange(VOX)[None, :]).astype(bf16)
    boundary = jnp.dot(pick, features, preferred_element_type=f32).astype(bf16)
    by_offset = jnp.transpose(weight, (1, 0, 2))
    beside, wall = pl.pallas_call(
        spread_kernel,
        out_shape=(
            jax.ShapeDtypeStruct((8, HC, CI), bf16),
            jax.ShapeDtypeStruct((NF, 2, KP // 2, IL, CO), bf16),
        ),
        in_specs=[VMEM] * 2,
        out_specs=(VMEM, VMEM),
        scratch_shapes=[dma(8), dma(8), dma(4), dma(4), dma(4), dma(4), dma(2)],
        compiler_params=pltpu.CompilerParams(collective_id=0, has_side_effects=True),
        name="spread",
    )(boundary, by_offset)
    s, f = lax.axis_index("space"), lax.axis_index("fsdp")

    def inside(sign):
        ok = [
            (s + sign * (a - 1) >= 0) & (s + sign * (a - 1) < NS) & (f + sign * (c - 1) >= 0) & (f + sign * (c - 1) < NF)
            for a, c in SIDES
        ]
        return jnp.stack(ok)[:, None, None]

    spots = jnp.where(neighbour_map >= VOX + 5 * HC, neighbour_map - HC, neighbour_map)
    conv_out, gw, own, halo = pl.pallas_call(
        compute_kernel,
        out_shape=(
            jax.ShapeDtypeStruct((VOX, CO), bf16),
            jax.ShapeDtypeStruct((NF, ROWS, CO), f32),
            jax.ShapeDtypeStruct((VOX, CI), f32),
            jax.ShapeDtypeStruct((8, HC, CI), f32),
        ),
        in_specs=[VMEM] * 6,
        out_specs=(VMEM,) * 4,
        scratch_shapes=[pltpu.VMEM((TAB, CI), bf16), pltpu.VMEM((TAB, 2 * CI), f32)],
        compiler_params=pltpu.CompilerParams(vmem_limit_bytes=40 << 20),
        name="stencil",
    )(features, beside, spots, spots.T, cotangent, wall)
    total, back = pl.pallas_call(
        reduce_kernel,
        out_shape=(
            jax.ShapeDtypeStruct((2, 2, NY, CHUNK, CO), f32),
            jax.ShapeDtypeStruct((8, HC, CI), f32),
        ),
        in_specs=[VMEM] * 2,
        out_specs=(VMEM, VMEM),
        scratch_shapes=[
            pltpu.VMEM((NF, HALF, CO), f32),
            pltpu.VMEM((NF, HALF, CO), f32),
            pltpu.VMEM((2, LINE, CO), f32),
            pltpu.VMEM((2, HALF, CO), f32),
            pltpu.VMEM((2, NY, CHUNK, CO), f32),
            pltpu.VMEM((2, NY, CHUNK, CO), f32),
            pltpu.VMEM((2, CHUNK, CO), f32),
            pltpu.VMEM((2, NZ, CHUNK, CO), f32),
        ]
        + [dma(8)] * 2 + [dma(NF)] * 2 + [dma(6)] * 2 + [pltpu.SemaphoreType.DMA((2, NY))] * 8,
        compiler_params=pltpu.CompilerParams(collective_id=1, has_side_effects=True, vmem_limit_bytes=40 << 20),
        name="reduce",
    )(gw, halo)
    incoming = jnp.sum(jnp.where(inside(-1), back, 0.0), 0)
    put = (jnp.arange(VOX)[:, None] == send_rows[None, :]).astype(f32)
    settled = own + jnp.dot(put, incoming, preferred_element_type=f32, precision=lax.Precision.HIGHEST)
    grad_weight = jnp.transpose(total.reshape(KP, IL, CO)[:KV], (1, 0, 2))
    return (conv_out, settled.astype(bf16), grad_weight)


def solution(mesh):
    rows = P(("space", "fsdp"), None)
    placed = (rows, rows, P("fsdp", None, None), P(None, ("space", "fsdp")), P(("space", "fsdp")))
    return jax.shard_map(
        body, mesh=mesh, in_specs=placed, out_specs=(rows, rows, P("fsdp", None, None)), check_vma=False
    )
```

time: 118 us -> 97.9 us (0.83)
  Pallas kernels: 106 us -> 88.2 us
    pallas_call x1, Pallas kernels: 70.2 us -> 51.1 us  [body(): pl.pallas_call(reduce_kernel, out_shape=(jax.ShapeDtypeStruct((2, 2, NY,...]
    pad x1 -> x0, local copies, waits for them, and re-layouts: 1.84 us -> none  [body(): jnp.pad(jnp.transpose(weight, (1, 0, 2)), ((0, 1), (0, 0), (0, 0)))]
    unnamed x9 -> x11, local copies, waits for them, and re-layouts: 3.91 us -> 4.85 us
where the time goes in v2:
time: 97.9 us; the launch traced here: 97.5 us
  Pallas kernels  88.2 us (90%)
  local copies, waits for them, and re-layouts  5.99 us (6%)
  matrix products  2.48 us (3%)
    pallas_call x1, Pallas kernels, body(): pl.pallas_call(reduce_kernel, out_shape=(jax.ShapeDtypeStruct((2, 2, NY,...  51.1 us
    pallas_call x1, Pallas kernels, body(): pl.pallas_call(spread_kernel, out_shape=(jax.ShapeDtypeStruct((8, HC, CI)...  28.9 us
    pallas_call x1, Pallas kernels, body(): pl.pallas_call(compute_kernel, out_shape=(jax.ShapeDtypeStruct((VOX, CO),...  8.19 us
    unnamed x11, local copies, waits for them, and re-layouts  4.85 us

profile of v2, /device:TPU:1, one launch (start us, length us, event | category | flops | bytes accessed | tf_op | source)
XLA Modules:
  0.0 97.5 jit_solution(8786573515848607159)
XLA Ops:
  0.6 1.7 %convolution_convert_fusion.b_ref = bf16[32,256]{1,0:T(8,128)(2,1)} fusion(bf16[128,256]{1,0:T(8,128)(2,1)} %feat_ref.1, s32[32]{0:T(128)} %param.9), kind=kOutput, calls=%fused_computation.2 | convolution fusion | flops 2109440 | bytes 82048 | tf_op jit(solution)/shard_map/dot_general | solution.py:286
  2.3 0.0 copy-start.4
  2.3 28.9 %spread.1 = (bf16[8,32,256]{2,1,0:T(8,128)(2,1)}, bf16[4,2,14,64,128]{4,3,2,1,0:T(8,128)(2,1)}) custom-call(bf16[32,256]{1,0:T(8,128)(2,1)} %convolution_convert_fusion.b_ref, bf16[27,64,128]{2,1,0:T(8,128)(2,1)} %bitcast.17), custom_call_target="tpu_custom_call" | custom-call | tf_op jit(solution)/shard_map/spread/pallas_call | solution.py:288
  31.2 0.8 copy.8
  32.0 0.1 copy.11.map_ref
  32.1 0.0 copy-start
  32.1 1.5 %copy-done = bf16[4,2,14,64,128]{4,3,2,1,0:T(8,128)(2,1)S(1)} copy-done((bf16[4,2,14,64,128]{4,3,2,1,0:T(8,128)(2,1)S(1)}, bf16[4,2,14,64,128]{4,3,2,1,0:T(8,128)(2,1)}, u32[]{:S(2)}) %copy-start) | copy-done | bytes 1835032
  33.6 0.0 copy-start.1
  33.6 0.9 copy-done.1
  34.5 0.0 copy-start.2
  34.5 0.8 copy-done.2
  35.4 0.0 copy-start.3
  35.4 0.8 copy-done.3
  36.1 8.2 %stencil.1 = (bf16[128,128]{1,0:T(8,128)(2,1)}, f32[4,1792,128]{2,1,0:T(8,128)S(1)}, f32[128,256]{1,0:T(8,128)S(1)}, f32[8,32,256]{2,1,0:T(8,128)S(1)}) custom-call(bf16[128,256]{1,0:T(8,128)(2,1)S(1)} %copy-done.2, bf16[8,32,256]{2,1,0:T(8,128)(2,1)S(1)} %copy-done.1, s32[27,128]{1,0:T(8,128)S(1)} %copy.11.map_ref, ...), custom_call_target="tpu_custom_call" | custom-call | tf_op jit(solution)/shard_map/stencil/pallas_call | solution.py:310
  44.3 51.1 %reduce.1 = (f32[2,2,8,56,128]{4,3,2,1,0:T(8,128)S(1)}, f32[8,32,256]{2,1,0:T(8,128)S(1)}) custom-call(f32[4,1792,128]{2,1,0:T(8,128)S(1)} %get-tuple-element.15.gw_ref, f32[8,32,256]{2,1,0:T(8,128)S(1)} %get-tuple-element.16.halo_ref), custom_call_target="tpu_custom_call" | custom-call | tf_op jit(solution)/shard_map/reduce/pallas_call | solution.py:324
  95.5 0.1 stack.35
  95.6 0.1 select_reduce_fusion
  95.7 0.0 copy-done.4
  95.7 0.8 fusion
  96.5 1.0 slice_bitcast_fusion
  (1 shorter events, 0.0 us)
Async XLA Ops:
  2.3 93.4 %copy-start.4 = (s32[32]{0:T(128)S(1)}, s32[32]{0:T(128)}, u32[]{:S(2)}) copy-start(s32[32]{0:T(128)} %param.9) | copy-start | bytes 388
  32.1 1.5 %copy-start = (bf16[4,2,14,64,128]{4,3,2,1,0:T(8,128)(2,1)S(1)}, bf16[4,2,14,64,128]{4,3,2,1,0:T(8,128)(2,1)}, u32[]{:S(2)}) copy-start(bf16[4,2,14,64,128]{4,3,2,1,0:T(8,128)(2,1)} %get-tuple-element.12.w_ref) | copy-start | bytes 5505028
  33.6 0.9 copy-start.1
  34.5 0.8 copy-start.2
  35.4 0.8 copy-start.3

commit v3 on v2

v3 whole, which is shorter than its diff:
```python
import math

import jax
import jax.numpy as jnp
from jax import lax
from jax.experimental import pallas as pl
from jax.experimental.pallas import tpu as pltpu
from jax.sharding import PartitionSpec as P

MESH = pl.DeviceIdType.MESH
VMEM = pl.BlockSpec(memory_space=pltpu.VMEM)
SIDES = [(a, c) for a in range(3) for c in range(3) if (a, c) != (1, 1)]
NS, NF, NY, NZ = 128, 4, 8, 8
VOX, HC, CI, CO, KV, KP = 128, 32, 256, 128, 27, 28
IL = CI // NF
ROWS = KP * IL
HALF = ROWS // 2
LINE = HALF // 2
SKIP = KV // 2
CHUNK = LINE // NY
PART = 112
TAB = VOX + 8 * HC


def position():
    s, f = lax.axis_index("space"), lax.axis_index("fsdp")
    core = lax.rem(s, 2)
    y = lax.rem(s // 2, NY)
    z = s // (2 * NY)
    return s, f, core, y, z


def shifted(s, f, ds, df):
    return (lax.rem(s + ds + NS, NS), lax.rem(f + df + NF, NF))


def meet(targets):
    barrier = pltpu.get_barrier_semaphore()
    for target in targets:
        pl.semaphore_signal(barrier, inc=1, device_id=target, device_id_type=MESH)
    pl.semaphore_wait(barrier, len(targets))


def remote(src, dst, send, recv, target):
    return pltpu.make_async_remote_copy(
        src_ref=src, dst_ref=dst, send_sem=send, recv_sem=recv, device_id=target, device_id_type=MESH
    )


def whole_kernel(b_ref, w_ref, feat_ref, map_ref, cot_ref, conv_ref, own_ref, total_ref, back_ref,
                 beside_ref, wall_ref, tab, tab_t, seen, gw_ref, tg, halo_ref, pbuf, acc0, rbuf, xbuf, acc1, ubuf, acc2, vbuf,
                 bs, br, ws, wr, hands, handr, own_sem,
                 hs, hr, ps, pr, xs, xr, us, ur, vs, vr, gs, gr, cs, cr):
    s, f, core, y, z = position()
    other = 1 - core
    partner = (s + 1 - 2 * core, f)
    left, right = shifted(s, f, 0, -1), shifted(s, f, 0, 1)
    from_left, from_right, opposite = left[1], right[1], lax.rem(f + 2, NF)

    def y_peer(d):
        return ((z * NY + lax.rem(y + d, NY)) * 2 + core, f)

    def z_peer(d):
        return ((lax.rem(z + d, NZ) * NY + y) * 2 + core, f)

    lines = ((y, y_peer), (z, z_peer))
    meet(
        [shifted(s, f, a - 1, c - 1) for a, c in SIDES]
        + [partner]
        + [y_peer(d) for d in range(1, NY)]
        + [z_peer(d) for d in range(1, NZ)]
    )
    spread = []
    for n, (a, c) in enumerate(SIDES):
        spread.append(remote(b_ref, beside_ref.at[n], bs.at[n], br.at[n], shifted(s, f, 1 - a, 1 - c)))
        spread[-1].start()
    own = [pltpu.make_async_copy(w_ref.at[pl.ds(h * SKIP, SKIP + 1)], wall_ref.at[f, h], own_sem.at[h]) for h in range(2)]
    own[0].start()
    own[1].start()
    quarter = KP // 4
    first, second = pl.ds(0, quarter), pl.ds(quarter, quarter)
    half_w = w_ref.at[pl.ds(core * SKIP, SKIP + 1)]
    wide = [
        remote(half_w, wall_ref.at[f, core], ws.at[0], wr.at[0], right),
        remote(half_w, wall_ref.at[f, core], ws.at[1], wr.at[1], left),
    ]
    wide[0].start()
    wide[1].start()

    def landed(side):
        return (
            wall_ref.at[from_left, side],
            wall_ref.at[from_right, side],
            wall_ref.at[opposite, side, first],
            wall_ref.at[opposite, side, second],
        )

    for copy in spread:
        copy.wait_recv()
    tab[:VOX, :] = feat_ref[...]
    for n, (a, c) in enumerate(SIDES):
        outer, inner = s + a - 1, f + c - 1
        ok = (outer >= 0) & (outer < NS) & (inner >= 0) & (inner < NF)
        rows_n = beside_ref[n]
        tab[VOX + n * HC : VOX + (n + 1) * HC, :] = jnp.where(ok, rows_n, jnp.zeros_like(rows_n))
    tab_t[...] = tab[...].T
    cot = cot_ref[...]
    rows = lax.broadcasted_iota(jnp.int32, (TAB, VOX), 0)
    scale = 1.0 / math.sqrt(NS * NF * VOX)

    def hot_of(k):
        return (rows == map_ref[k]).astype(jnp.bfloat16)

    def weight_half(side):
        def step(i, _):
            for u in range(2):
                k = side * (KP // 2) + 2 * i + u
                picked = jnp.dot(tab_t[...], hot_of(k), preferred_element_type=jnp.float32).astype(jnp.bfloat16)
                seen[k] = picked
                gw = jnp.dot(picked, cot, preferred_element_type=jnp.float32) * scale
                for q in range(NF):
                    gw_ref[q, pl.ds(pl.multiple_of(k * IL, IL), IL), :] = gw[q * IL : (q + 1) * IL]
            return 0

        lax.fori_loop(0, KP // 4, step, 0)

    weight_half(other)
    order = (2, 1, 3, 0)
    pairs = {}
    for d in order:
        src = gw_ref.at[lax.rem(f + d, NF), pl.ds(other * HALF, HALF), :]
        pairs[d] = remote(src, pbuf.at[d], ps.at[d], pr.at[d], partner)
        pairs[d].start()
    weight_half(core)
    passed = []
    for m, got in enumerate(landed(core)):
        remote(got, got, ws.at[m], wr.at[m], partner).wait_recv()
        if m == 0:
            piece = wall_ref.at[from_left, core, first]
            wide.append(remote(piece, piece, ws.at[2], wr.at[2], right))
            wide[-1].start()
        if m == 1:
            piece = wall_ref.at[from_right, core, second]
            wide.append(remote(piece, piece, ws.at[3], wr.at[3], left))
            wide[-1].start()
        passed.append(remote(got, got, hands.at[m], handr.at[m], partner))
        passed[-1].start()
    half_a, half_b = pl.ds(0, LINE), pl.ds(LINE, LINE)
    across = {}

    def send_x(m, src, dst, target):
        across[m] = remote(src, dst, xs.at[m], xr.at[m], target)
        across[m].start()

    for d in order:
        j = lax.rem(f + d, NF)
        pairs[d].wait_recv()

        def add_pair(i, _):
            here = pl.ds(pl.multiple_of(i * PART, 8), PART)
            mine = pl.ds(pl.multiple_of(core * HALF + i * PART, 8), PART)
            acc0[d, here, :] = gw_ref[j, mine, :] + pbuf[d, here, :]
            return 0

        lax.fori_loop(0, HALF // PART, add_pair, 0)
        if d == 2:
            send_x(0, acc0.at[2, half_a], rbuf.at[0], right)
            send_x(1, acc0.at[2, half_b], rbuf.at[1], left)
        if d == 1:
            send_x(2, acc0.at[1, half_b], xbuf.at[0, half_b], right)
        if d == 3:
            send_x(3, acc0.at[3, half_a], xbuf.at[1, half_a], left)

    for m, d, begin, half, target in ((0, 1, 0, half_a, right), (1, 3, LINE, half_b, left)):
        across[m].wait_recv()

        def add_relay(i, _):
            here = pl.ds(pl.multiple_of(begin + i * PART, 8), PART)
            acc0[d, here, :] += rbuf[m, pl.ds(pl.multiple_of(i * PART, 8), PART), :]
            return 0

        lax.fori_loop(0, LINE // PART, add_relay, 0)
        send_x(4 + m, acc0.at[d, half], xbuf.at[m, half], target)

    for m, there in enumerate(landed(other)):
        remote(there, there, hands.at[m], handr.at[m], partner).wait_recv()
    own[0].wait()
    own[1].wait()
    tg[...] = jnp.zeros_like(tg)

    def spread_group(g, acc):
        hot, high, low = [], [], []
        for u in range(3):
            k = g * 3 + u
            side = k // (SKIP + 1)
            kernel = wall_ref[:, side, k - side * SKIP].reshape(CI, CO)
            acc = acc + lax.dot_general(seen[k], kernel, (((0,), (0,)), ((), ())), preferred_element_type=jnp.float32)
            term = lax.dot_general(cot, kernel, (((1,), (1,)), ((), ())), preferred_element_type=jnp.float32)
            top = term.astype(jnp.bfloat16)
            high.append(top)
            low.append((term - top.astype(jnp.float32)).astype(jnp.bfloat16))
            hot.append(hot_of(k))
        both = jnp.concatenate([jnp.concatenate(high, 0), jnp.concatenate(low, 0)], 1)
        tg[...] += jnp.dot(jnp.concatenate(hot, 1), both, preferred_element_type=jnp.float32)
        return acc

    acc = lax.fori_loop(0, KV // 3, spread_group, jnp.zeros((VOX, CO), jnp.float32))
    conv_ref[...] = acc.astype(jnp.bfloat16)
    own_ref[...] = tg[:VOX, :CI] + tg[:VOX, CI:]
    halo_ref[...] = (tg[VOX:, :CI] + tg[VOX:, CI:]).reshape(8, HC, CI)
    copies = []
    for n, (a, c) in enumerate(SIDES):
        copies.append(remote(halo_ref.at[n], back_ref.at[n], hs.at[n], hr.at[n], shifted(s, f, a - 1, c - 1)))
        copies[-1].start()
    u_copies = []
    for t, needs in enumerate(((3, 4), (2, 5))):
        for m in needs:
            across[m].wait_recv()

        def add_x(i, _):
            here = pl.ds(pl.multiple_of(t * LINE + i * CHUNK, 8), CHUNK)
            acc1[t, i] = acc0[0, here, :] + (xbuf[0, here, :] + xbuf[1, here, :])
            return 0

        lax.fori_loop(0, NY, add_x, 0)
        at, peer = lines[t]
        for d in range(1, NY):
            u_copies.append(remote(acc1.at[t, lax.rem(at + d, NY)], ubuf.at[t, d], us.at[t, d], ur.at[t, d], peer(d)))
            u_copies[-1].start()
    v_copies = []
    for t in range(2):
        for copy in u_copies[t * 7 : t * 7 + 7]:
            copy.wait_recv()
        running = acc1[t, lines[t][0]]
        for d in range(1, NY):
            running = running + ubuf[t, d]
        acc2[t] = running
        at, peer = lines[1 - t]
        vbuf[t, at] = running
        for d in range(1, NZ):
            v_copies.append(remote(acc2.at[t], vbuf.at[t, at], vs.at[t, d], vr.at[t, d], peer(d)))
            v_copies[-1].start()
    g_copies, handed = [], []
    for t in range(2):
        across_at = lines[1 - t][0]
        for d in range(1, NZ):
            got = vbuf.at[t, lax.rem(across_at - d + NZ, NZ)]
            remote(got, got, vs.at[t, d], vr.at[t, d], partner).wait_recv()
        done = vbuf[t, 0]
        for q in range(1, NZ):
            done = done + vbuf[t, q]
        at, peer = lines[t]
        total_ref[core, t, at] = done
        mine = total_ref.at[core, t, at]
        for d in range(1, NY):
            g_copies.append(remote(mine, mine, gs.at[t, d], gr.at[t, d], peer(d)))
            g_copies[-1].start()
        handed.append(remote(mine, mine, cs.at[t, 0], cr.at[t, 0], partner))
        handed[-1].start()
    for copy in copies:
        copy.wait()
    for d in range(1, NY):
        for t in range(2):
            got = total_ref.at[core, t, lax.rem(lines[t][0] - d + NY, NY)]
            remote(got, got, gs.at[t, d], gr.at[t, d], partner).wait_recv()
            handed.append(remote(got, got, cs.at[t, d], cr.at[t, d], partner))
            handed[-1].start()
    for d in range(NY):
        for t in range(2):
            there = total_ref.at[other, t, lax.rem(lines[t][0] - d + NY, NY)]
            remote(there, there, cs.at[t, d], cr.at[t, d], partner).wait_recv()
    for copy in handed + u_copies + v_copies + g_copies:
        copy.wait_send()
    for d in order:
        pairs[d].wait_send()
    for m in range(6):
        across[m].wait_send()
    for copy in passed + wide + spread:
        copy.wait_send()


def dma(*shape):
    return pltpu.SemaphoreType.DMA(shape)


def body(features, cotangent, weight, neighbour_map, send_rows):
    f32, bf16 = jnp.float32, jnp.bfloat16
    pick = (send_rows[:, None] == jnp.arange(VOX)[None, :]).astype(bf16)
    boundary = jnp.dot(pick, features, preferred_element_type=f32).astype(bf16)
    by_offset = jnp.transpose(weight, (1, 0, 2))
    spots = jnp.where(neighbour_map >= VOX + 5 * HC, neighbour_map - HC, neighbour_map)
    spots = jnp.pad(spots, ((0, 1), (0, 0)), constant_values=TAB).reshape(KP, 1, VOX)
    conv_out, own, total, back = pl.pallas_call(
        whole_kernel,
        out_shape=(
            jax.ShapeDtypeStruct((VOX, CO), bf16),
            jax.ShapeDtypeStruct((VOX, CI), f32),
            jax.ShapeDtypeStruct((2, 2, NY, CHUNK, CO), f32),
            jax.ShapeDtypeStruct((8, HC, CI), f32),
        ),
        in_specs=[VMEM] * 5,
        out_specs=(VMEM,) * 4,
        scratch_shapes=[
            pltpu.VMEM((8, HC, CI), bf16),
            pltpu.VMEM((NF, 2, KP // 2, IL, CO), bf16),
            pltpu.VMEM((TAB, CI), bf16),
            pltpu.VMEM((CI, TAB), bf16),
            pltpu.VMEM((KP, CI, VOX), bf16),
            pltpu.VMEM((NF, ROWS, CO), f32),
            pltpu.VMEM((TAB, 2 * CI), f32),
            pltpu.VMEM((8, HC, CI), f32),
            pltpu.VMEM((NF, HALF, CO), f32),
            pltpu.VMEM((NF, HALF, CO), f32),
            pltpu.VMEM((2, LINE, CO), f32),
            pltpu.VMEM((2, HALF, CO), f32),
            pltpu.VMEM((2, NY, CHUNK, CO), f32),
            pltpu.VMEM((2, NY, CHUNK, CO), f32),
            pltpu.VMEM((2, CHUNK, CO), f32),
            pltpu.VMEM((2, NZ, CHUNK, CO), f32),
            dma(8), dma(8), dma(4), dma(4), dma(4), dma(4), dma(2),
        ]
        + [dma(8)] * 2 + [dma(NF)] * 2 + [dma(6)] * 2 + [dma(2, NY)] * 8,
        compiler_params=pltpu.CompilerParams(collective_id=0, has_side_effects=True, vmem_limit_bytes=48 << 20),
        name="whole",
    )(boundary, by_offset, features, spots, cotangent)
    s, f = lax.axis_index("space"), lax.axis_index("fsdp")

    def inside(sign):
        ok = [
            (s + sign * (a - 1) >= 0) & (s + sign * (a - 1) < NS) & (f + sign * (c - 1) >= 0) & (f + sign * (c - 1) < NF)
            for a, c in SIDES
        ]
        return jnp.stack(ok)[:, None, None]

    incoming = jnp.sum(jnp.where(inside(-1), back, 0.0), 0)
    put = (jnp.arange(VOX)[:, None] == send_rows[None, :]).astype(f32)
    settled = own + jnp.dot(put, incoming, preferred_element_type=f32, precision=lax.Precision.HIGHEST)
    grad_weight = jnp.transpose(total.reshape(KP, IL, CO)[:KV], (1, 0, 2))
    return (conv_out, settled.astype(bf16), grad_weight)


def solution(mesh):
    rows = P(("space", "fsdp"), None)
    placed = (rows, rows, P("fsdp", None, None), P(None, ("space", "fsdp")), P(("space", "fsdp")))
    return jax.shard_map(
        body, mesh=mesh, in_specs=placed, out_specs=(rows, rows, P("fsdp", None, None)), check_vma=False
    )
```

time: 97.9 us -> 79.5 us (0.81)
  Pallas kernels: 88.2 us -> 72.9 us
  local copies, waits for them, and re-layouts: 5.99 us -> 4.52 us
  matrix products: 2.48 us -> 1.01 us
    pallas_call x3 -> x1, Pallas kernels: 88.2 us -> 72.9 us  [body(): pl.pallas_call(whole_kernel, out_shape=(jax.ShapeDtypeStruct((VOX, CO), b...]
    dot_general x1, matrix products: 1.65 us -> 0.18 us  [body(): boundary = jnp.dot(pick, features, preferred_element_type=f32).astype(bf16)]
    unnamed x11, local copies, waits for them, and re-layouts: 4.85 us -> 3.42 us
where the time goes in v3:
time: 79.5 us; the launch traced here: 79.3 us
  Pallas kernels  72.9 us (92%)
  local copies, waits for them, and re-layouts  4.52 us (6%)
  matrix products  1.01 us (1%)
    pallas_call x1, Pallas kernels, body(): pl.pallas_call(whole_kernel, out_shape=(jax.ShapeDtypeStruct((VOX, CO), b...  72.9 us
    unnamed x11, local copies, waits for them, and re-layouts  3.42 us

profile of v3, /device:TPU:1, one launch (start us, length us, event | category | flops | bytes accessed | tf_op | source)
XLA Modules:
  0.0 79.3 jit_solution(7861351949298036519)
XLA Ops:
  0.7 0.0 copy-start.3
  0.7 0.0 copy-start.1
  0.7 0.1 stack.35
  0.8 0.6 copy-done.3
  1.4 0.0 copy-start.4
  1.4 0.1 copy-done.1
  1.5 0.5 copy-done.4
  2.0 0.0 copy-start.2
  2.1 0.2 convolution_convert_fusion.b_ref
  2.2 0.6 copy-done.2
  2.8 0.0 copy-start
  2.8 1.0 %copy-done = bf16[64,27,128]{2,0,1:T(8,128)(2,1)S(1)} copy-done((bf16[64,27,128]{2,0,1:T(8,128)(2,1)S(1)}, bf16[64,27,128]{2,0,1:T(8,128)(2,1)}, u32[]{:S(2)}) %copy-start) | copy-done | bytes 442392
  3.8 72.9 %whole.1 = (bf16[128,128]{1,0:T(8,128)(2,1)S(1)}, f32[128,256]{1,0:T(8,128)S(1)}, f32[2,2,8,56,128]{4,3,2,1,0:T(8,128)S(1)}, f32[8,32,256]{2,1,0:T(8,128)S(1)}) custom-call(bf16[32,256]{1,0:T(8,128)(2,1)S(1)} %convolution_convert_fusion.b_ref, bf16[27,64,128]{2,1,0:T(8,128)(2,1)S(1)} %bitcast.15, bf16[128,256]{1,0:T(8,128)(2,1)S(1)} %copy-done.1, ...), custom_call_target="tpu_custom_call" | custom-call | tf_op jit(solution)/shard_map/whole/pallas_call | solution.py:293
  76.7 0.1 select_reduce_fusion
  76.8 0.8 %fusion = bf16[128,256]{1,0:T(8,128)(2,1)} fusion(f32[128,256]{1,0:T(8,128)S(1)} %get-tuple-element.8, f32[32,256]{1,0:T(8,128)S(1)} %select_reduce_fusion, s32[32]{0:T(128)S(1)} %copy-done.4), kind=kOutput, calls=%fused_computation.1 | convolution fusion | flops 12652544 | bytes 229504 | tf_op jit(solution)/shard_map/dot_general | solution.py:337
  77.7 1.0 %slice_bitcast_fusion = f32[64,27,128]{2,0,1:T(8,128)} fusion(f32[28,64,128]{2,1,0:T(8,128)S(1)} %bitcast.14), kind=kLoop, calls=%fused_computation.3 | loop fusion | bytes 1769472 | tf_op jit(solution)/shard_map/transpose | solution.py:338
  78.6 0.6 copy.9
  (3 shorter events, 0.0 us)
Async XLA Ops:
  0.7 0.7 copy-start.3
  0.7 0.8 %copy-start.1 = (bf16[128,256]{1,0:T(8,128)(2,1)S(1)}, bf16[128,256]{1,0:T(8,128)(2,1)}, u32[]{:S(2)}) copy-start(bf16[128,256]{1,0:T(8,128)(2,1)} %feat_ref.1) | copy-start | bytes 196612
  1.4 0.7 copy-start.4
  2.0 0.8 copy-start.2
  2.8 1.0 %copy-start = (bf16[64,27,128]{2,0,1:T(8,128)(2,1)S(1)}, bf16[64,27,128]{2,0,1:T(8,128)(2,1)}, u32[]{:S(2)}) copy-start(bf16[64,27,128]{2,0,1:T(8,128)(2,1)} %param.7) | copy-start | bytes 1327108

commit v4 on v3

--- a/solution.py
+++ b/solution.py
@@ -17,7 +17,9 @@
 HALF = ROWS // 2
 LINE = HALF // 2
 SKIP = KV // 2
-CHUNK = LINE // NY
+BIG, SMALL = 32, 24
+SEGMENTS = ((0, 0, BIG), (1, LINE, BIG), (0, NY * BIG, SMALL), (1, LINE + NY * BIG, SMALL))
+FAR_FIRST = (4, 3, 5, 2, 6, 1, 7)
 PART = 112
 TAB = VOX + 8 * HC
 
@@ -145,12 +147,14 @@
             wide[-1].start()
         passed.append(remote(got, got, hands.at[m], handr.at[m], partner))
         passed[-1].start()
-    half_a, half_b = pl.ds(0, LINE), pl.ds(LINE, LINE)
     across = {}
 
-    def send_x(m, src, dst, target):
-        across[m] = remote(src, dst, xs.at[m], xr.at[m], target)
-        across[m].start()
+    def rows_of(g):
+        return pl.ds(SEGMENTS[g][1], NY * SEGMENTS[g][2])
+
+    def send_x(m, h, src, dst, target):
+        across[m, h] = remote(src, dst, xs.at[m, h], xr.at[m, h], target)
+        across[m, h].start()
 
     for d in order:
         j = lax.rem(f + d, NF)
@@ -164,24 +168,56 @@
 
         lax.fori_loop(0, HALF // PART, add_pair, 0)
         if d == 2:
-            send_x(0, acc0.at[2, half_a], rbuf.at[0], right)
-            send_x(1, acc0.at[2, half_b], rbuf.at[1], left)
+            for h in range(2):
+                send_x(0, h, acc0.at[2, rows_of(2 * h)], rbuf.at[rows_of(2 * h)], right)
+                send_x(1, h, acc0.at[2, rows_of(2 * h + 1)], rbuf.at[rows_of(2 * h + 1)], left)
         if d == 1:
-            send_x(2, acc0.at[1, half_b], xbuf.at[0, half_b], right)
+            send_x(2, 0, acc0.at[1, rows_of(1)], xbuf.at[0, rows_of(1)], right)
         if d == 3:
-            send_x(3, acc0.at[3, half_a], xbuf.at[1, half_a], left)
-
-    for m, d, begin, half, target in ((0, 1, 0, half_a, right), (1, 3, LINE, half_b, left)):
-        across[m].wait_recv()
-
-        def add_relay(i, _):
-            here = pl.ds(pl.multiple_of(begin + i * PART, 8), PART)
-            acc0[d, here, :] += rbuf[m, pl.ds(pl.multiple_of(i * PART, 8), PART), :]
+            send_x(3, 0, acc0.at[3, rows_of(0)], xbuf.at[1, rows_of(0)], left)
+
+    for h in range(2):
+        if h == 1:
+            send_x(2, 1, acc0.at[1, rows_of(3)], xbuf.at[0, rows_of(3)], right)
+            send_x(3, 1, acc0.at[3, rows_of(2)], xbuf.at[1, rows_of(2)], left)
+        for m, d, target in ((0, 1, right), (1, 3, left)):
+            across[m, h].wait_recv()
+            t, begin, size = SEGMENTS[2 * h + m]
+
+            def add_relay(i, _):
+                here = pl.ds(pl.multiple_of(begin + i * 2 * size, 8), 2 * size)
+                acc0[d, here, :] += rbuf[here, :]
+                return 0
+
+            lax.fori_loop(0, NY // 2, add_relay, 0)
+            send_x(4 + m, h, acc0.at[d, rows_of(2 * h + m)], xbuf.at[m, rows_of(2 * h + m)], target)
+
+    def part(ref, g, p):
+        t, begin, size = SEGMENTS[g]
+        return ref.at[g, p, pl.ds(0, size)]
+
+    u_copies, v_copies, g_copies, handed = {}, [], [], []
+
+    def enter(g):
+        t, begin, size = SEGMENTS[g]
+        for m in ((3, 4), (2, 5))[t]:
+            across[m, g // 2].wait_recv()
+
+        def add_x(i, _):
+            here = pl.ds(pl.multiple_of(begin + i * size, 8), size)
+            acc1[g, i, :size] = acc0[0, here, :] + (xbuf[0, here, :] + xbuf[1, here, :])
             return 0
 
-        lax.fori_loop(0, LINE // PART, add_relay, 0)
-        send_x(4 + m, acc0.at[d, half], xbuf.at[m, half], target)
-
+        lax.fori_loop(0, NY, add_x, 0)
+        at, peer = lines[t]
+        for d in FAR_FIRST:
+            u_copies[g, d] = remote(
+                part(acc1, g, lax.rem(at + d, NY)), part(ubuf, g, d), us.at[g, d], ur.at[g, d], peer(d)
+            )
+            u_copies[g, d].start()
+
+    enter(0)
+    enter(1)
     for m, there in enumerate(landed(other)):
         remote(there, there, hands.at[m], handr.at[m], partner).wait_recv()
     own[0].wait()
@@ -212,69 +248,60 @@
     for n, (a, c) in enumerate(SIDES):
         copies.append(remote(halo_ref.at[n], back_ref.at[n], hs.at[n], hr.at[n], shifted(s, f, a - 1, c - 1)))
         copies[-1].start()
-    u_copies = []
-    for t, needs in enumerate(((3, 4), (2, 5))):
-        for m in needs:
-            across[m].wait_recv()
-
-        def add_x(i, _):
-            here = pl.ds(pl.multiple_of(t * LINE + i * CHUNK, 8), CHUNK)
-            acc1[t, i] = acc0[0, here, :] + (xbuf[0, here, :] + xbuf[1, here, :])
-            return 0
-
-        lax.fori_loop(0, NY, add_x, 0)
-        at, peer = lines[t]
+    enter(2)
+    enter(3)
+    for g, (t, begin, size) in enumerate(SEGMENTS):
+        running = acc1[g, lines[t][0], :size]
         for d in range(1, NY):
-            u_copies.append(remote(acc1.at[t, lax.rem(at + d, NY)], ubuf.at[t, d], us.at[t, d], ur.at[t, d], peer(d)))
-            u_copies[-1].start()
-    v_copies = []
-    for t in range(2):
-        for copy in u_copies[t * 7 : t * 7 + 7]:
-            copy.wait_recv()
-        running = acc1[t, lines[t][0]]
-        for d in range(1, NY):
-            running = running + ubuf[t, d]
-        acc2[t] = running
+            u_copies[g, d].wait_recv()
+            running = running + ubuf[g, d, :size]
+        acc2[g, :size] = running
         at, peer = lines[1 - t]
-        vbuf[t, at] = running
-        for d in range(1, NZ):
-            v_copies.append(remote(acc2.at[t], vbuf.at[t, at], vs.at[t, d], vr.at[t, d], peer(d)))
+        vbuf[g, at, :size] = running
+        for d in FAR_FIRST:
+            v_copies.append(
+                remote(acc2.at[g, pl.ds(0, size)], part(vbuf, g, at), vs.at[g, d], vr.at[g, d], peer(d))
+            )
             v_copies[-1].start()
-    g_copies, handed = [], []
-    for t in range(2):
+
+    def spot(side, g, p):
+        t, begin, size = SEGMENTS[g]
+        return pl.ds(pl.multiple_of(side * HALF + begin + p * size, 8), size)
+
+    for g, (t, begin, size) in enumerate(SEGMENTS):
         across_at = lines[1 - t][0]
         for d in range(1, NZ):
-            got = vbuf.at[t, lax.rem(across_at - d + NZ, NZ)]
-            remote(got, got, vs.at[t, d], vr.at[t, d], partner).wait_recv()
-        done = vbuf[t, 0]
+            got = part(vbuf, g, lax.rem(across_at - d + NZ, NZ))
+            remote(got, got, vs.at[g, d], vr.at[g, d], partner).wait_recv()
+        done = vbuf[g, 0, :size]
         for q in range(1, NZ):
-            done = done + vbuf[t, q]
+            done = done + vbuf[g, q, :size]
         at, peer = lines[t]
-        total_ref[core, t, at] = done
-        mine = total_ref.at[core, t, at]
-        for d in range(1, NY):
-            g_copies.append(remote(mine, mine, gs.at[t, d], gr.at[t, d], peer(d)))
+        total_ref[spot(core, g, at), :] = done
+        mine = total_ref.at[spot(core, g, at)]
+        for d in FAR_FIRST:
+            g_copies.append(remote(mine, mine, gs.at[g, d], gr.at[g, d], peer(d)))
             g_copies[-1].start()
-        handed.append(remote(mine, mine, cs.at[t, 0], cr.at[t, 0], partner))
+        handed.append(remote(mine, mine, cs.at[g, 0], cr.at[g, 0], partner))
         handed[-1].start()
     for copy in copies:
         copy.wait()
-    for d in range(1, NY):
-        for t in range(2):
-            got = total_ref.at[core, t, lax.rem(lines[t][0] - d + NY, NY)]
-            remote(got, got, gs.at[t, d], gr.at[t, d], partner).wait_recv()
-            handed.append(remote(got, got, cs.at[t, d], cr.at[t, d], partner))
+    for g, (t, begin, size) in enumerate(SEGMENTS):
+        for d in (1, 7, 2, 6, 3, 5, 4):
+            got = total_ref.at[spot(core, g, lax.rem(lines[t][0] - d + NY, NY))]
+            remote(got, got, gs.at[g, d], gr.at[g, d], partner).wait_recv()
+            handed.append(remote(got, got, cs.at[g, d], cr.at[g, d], partner))
             handed[-1].start()
-    for d in range(NY):
-        for t in range(2):
-            there = total_ref.at[other, t, lax.rem(lines[t][0] - d + NY, NY)]
-            remote(there, there, cs.at[t, d], cr.at[t, d], partner).wait_recv()
-    for copy in handed + u_copies + v_copies + g_copies:
+    for g, (t, begin, size) in enumerate(SEGMENTS):
+        for d in range(NY):
+            there = total_ref.at[spot(other, g, lax.rem(lines[t][0] - d + NY, NY))]
+            remote(there, there, cs.at[g, d], cr.at[g, d], partner).wait_recv()
+    for copy in handed + list(u_copies.values()) + v_copies + g_copies:
         copy.wait_send()
     for d in order:
         pairs[d].wait_send()
-    for m in range(6):
-        across[m].wait_send()
+    for copy in across.values():
+        copy.wait_send()
     for copy in passed + wide + spread:
         copy.wait_send()
 
@@ -295,7 +322,7 @@
         out_shape=(
             jax.ShapeDtypeStruct((VOX, CO), bf16),
             jax.ShapeDtypeStruct((VOX, CI), f32),
-            jax.ShapeDtypeStruct((2, 2, NY, CHUNK, CO), f32),
+            jax.ShapeDtypeStruct((ROWS, CO), f32),
             jax.ShapeDtypeStruct((8, HC, CI), f32),
         ),
         in_specs=[VMEM] * 5,
@@ -311,15 +338,15 @@
             pltpu.VMEM((8, HC, CI), f32),
             pltpu.VMEM((NF, HALF, CO), f32),
             pltpu.VMEM((NF, HALF, CO), f32),
-            pltpu.VMEM((2, LINE, CO), f32),
+            pltpu.VMEM((HALF, CO), f32),
             pltpu.VMEM((2, HALF, CO), f32),
-            pltpu.VMEM((2, NY, CHUNK, CO), f32),
-            pltpu.VMEM((2, NY, CHUNK, CO), f32),
-            pltpu.VMEM((2, CHUNK, CO), f32),
-            pltpu.VMEM((2, NZ, CHUNK, CO), f32),
+            pltpu.VMEM((4, NY, BIG, CO), f32),
+            pltpu.VMEM((4, NY, BIG, CO), f32),
+            pltpu.VMEM((4, BIG, CO), f32),
+            pltpu.VMEM((4, NZ, BIG, CO), f32),
             dma(8), dma(8), dma(4), dma(4), dma(4), dma(4), dma(2),
         ]
-        + [dma(8)] * 2 + [dma(NF)] * 2 + [dma(6)] * 2 + [dma(2, NY)] * 8,
+        + [dma(8)] * 2 + [dma(NF)] * 2 + [dma(6, 2)] * 2 + [dma(4, NY)] * 8,
         compiler_params=pltpu.CompilerParams(collective_id=0, has_side_effects=True, vmem_limit_bytes=48 << 20),
         name="whole",
     )(boundary, by_offset, features, spots, cotangent)

time: 79.5 us -> 78.3 us (0.985)
  Pallas kernels: 72.9 us -> 71.7 us
    pallas_call x1, Pallas kernels: 72.9 us -> 71.7 us  [body(): pl.pallas_call(whole_kernel, out_shape=(jax.ShapeDtypeStruct((VOX, CO), b...]
    transpose x1 -> x0, local copies, waits for them, and re-layouts: 0.97 us -> none  [body(): grad_weight = jnp.transpose(total.reshape(KP, IL, CO)[:KV], (1, 0, 2))]
    slice x0 -> x1, local copies, waits for them, and re-layouts: none -> 0.97 us  [body(): grad_weight = jnp.transpose(total.reshape(KP, IL, CO)[:KV], (1, 0, 2))]
where the time goes in v4:
time: 78.3 us; the launch traced here: 78.1 us
  Pallas kernels  71.7 us (92%)
  local copies, waits for them, and re-layouts  4.52 us (6%)
  matrix products  1.01 us (1%)
    pallas_call x1, Pallas kernels, body(): pl.pallas_call(whole_kernel, out_shape=(jax.ShapeDtypeStruct((VOX, CO), b...  71.7 us
    unnamed x11, local copies, waits for them, and re-layouts  3.42 us

profile of v4, /device:TPU:1, one launch (start us, length us, event | category | flops | bytes accessed | tf_op | source)
XLA Modules:
  0.0 78.1 jit_solution(8163385142553408198)
XLA Ops:
  0.7 0.0 copy-start.3
  0.7 0.0 copy-start.1
  0.7 0.1 stack.35
  0.8 0.6 copy-done.3
  1.4 0.0 copy-start.4
  1.4 0.1 copy-done.1
  1.5 0.5 copy-done.4
  2.0 0.0 copy-start.2
  2.1 0.2 convolution_convert_fusion.b_ref
  2.2 0.6 copy-done.2
  2.8 0.0 copy-start
  2.8 1.0 %copy-done = bf16[64,27,128]{2,0,1:T(8,128)(2,1)S(1)} copy-done((bf16[64,27,128]{2,0,1:T(8,128)(2,1)S(1)}, bf16[64,27,128]{2,0,1:T(8,128)(2,1)}, u32[]{:S(2)}) %copy-start) | copy-done | bytes 442392
  3.8 71.7 %whole.1 = (bf16[128,128]{1,0:T(8,128)(2,1)S(1)}, f32[128,256]{1,0:T(8,128)S(1)}, f32[1792,128]{1,0:T(8,128)S(1)}, f32[8,32,256]{2,1,0:T(8,128)S(1)}) custom-call(bf16[32,256]{1,0:T(8,128)(2,1)S(1)} %convolution_convert_fusion.b_ref, bf16[27,64,128]{2,1,0:T(8,128)(2,1)S(1)} %bitcast.14, bf16[128,256]{1,0:T(8,128)(2,1)S(1)} %copy-done.1, ...), custom_call_target="tpu_custom_call" | custom-call | tf_op jit(solution)/shard_map/whole/pallas_call | solution.py:320
  75.5 0.1 select_reduce_fusion
  75.6 0.8 %fusion = bf16[128,256]{1,0:T(8,128)(2,1)} fusion(f32[128,256]{1,0:T(8,128)S(1)} %get-tuple-element.8, f32[32,256]{1,0:T(8,128)S(1)} %select_reduce_fusion, s32[32]{0:T(128)S(1)} %copy-done.4), kind=kOutput, calls=%fused_computation.1 | convolution fusion | flops 12652544 | bytes 229504 | tf_op jit(solution)/shard_map/dot_general | solution.py:364
  76.5 1.0 %slice.6 = f32[1728,128]{1,0:T(8,128)} slice(f32[1792,128]{1,0:T(8,128)S(1)} %get-tuple-element.10), slice={[0:1728], [0:128]} | slice | bytes 1769472 | tf_op jit(solution)/shard_map/slice | solution.py:365
  77.4 0.6 copy.9
  (3 shorter events, 0.0 us)
Async XLA Ops:
  0.7 0.7 copy-start.3
  0.7 0.8 %copy-start.1 = (bf16[128,256]{1,0:T(8,128)(2,1)S(1)}, bf16[128,256]{1,0:T(8,128)(2,1)}, u32[]{:S(2)}) copy-start(bf16[128,256]{1,0:T(8,128)(2,1)} %feat_ref.1) | copy-start | bytes 196612
  1.4 0.7 copy-start.4
  2.0 0.8 copy-start.2
  2.8 1.0 %copy-start = (bf16[64,27,128]{2,0,1:T(8,128)(2,1)S(1)}, bf16[64,27,128]{2,0,1:T(8,128)(2,1)}, u32[]{:S(2)}) copy-start(bf16[64,27,128]{2,0,1:T(8,128)(2,1)} %param.7) | copy-start | bytes 1327108

commit v5 on v4

--- a/solution.py
+++ b/solution.py
@@ -17,6 +17,7 @@
 HALF = ROWS // 2
 LINE = HALF // 2
 SKIP = KV // 2
+BATCH = 7
 BIG, SMALL = 32, 24
 SEGMENTS = ((0, 0, BIG), (1, LINE, BIG), (0, NY * BIG, SMALL), (1, LINE + NY * BIG, SMALL))
 FAR_FIRST = (4, 3, 5, 2, 6, 1, 7)
@@ -49,8 +50,8 @@
     )
 
 
-def whole_kernel(b_ref, w_ref, feat_ref, map_ref, cot_ref, conv_ref, own_ref, total_ref, back_ref,
-                 beside_ref, wall_ref, tab, tab_t, seen, gw_ref, tg, halo_ref, pbuf, acc0, rbuf, xbuf, acc1, ubuf, acc2, vbuf,
+def whole_kernel(b_ref, w_ref, feat_in, map_in, cot_in, conv_ref, own_ref, total_ref, back_ref,
+                 map_ref, cot_ref, in_sem, beside_ref, wall_ref, tab, tab_t, seen, gw_ref, tg, halo_ref, pbuf, acc0, rbuf, xbuf, acc1, ubuf, acc2, vbuf,
                  bs, br, ws, wr, hands, handr, own_sem,
                  hs, hr, ps, pr, xs, xr, us, ur, vs, vr, gs, gr, cs, cr):
     s, f, core, y, z = position()
@@ -66,6 +67,13 @@
         return ((lax.rem(z + d, NZ) * NY + y) * 2 + core, f)
 
     lines = ((y, y_peer), (z, z_peer))
+    taken = [
+        pltpu.make_async_copy(feat_in, tab.at[pl.ds(0, VOX)], in_sem.at[0]),
+        pltpu.make_async_copy(map_in, map_ref, in_sem.at[1]),
+        pltpu.make_async_copy(cot_in, cot_ref, in_sem.at[2]),
+    ]
+    for copy in taken:
+        copy.start()
     meet(
         [shifted(s, f, a - 1, c - 1) for a, c in SIDES]
         + [partner]
@@ -99,7 +107,8 @@
 
     for copy in spread:
         copy.wait_recv()
-    tab[:VOX, :] = feat_ref[...]
+    for copy in taken:
+        copy.wait()
     for n, (a, c) in enumerate(SIDES):
         outer, inner = s + a - 1, f + c - 1
         ok = (outer >= 0) & (outer < NS) & (inner >= 0) & (inner < NF)
@@ -115,16 +124,19 @@
 
     def weight_half(side):
         def step(i, _):
-            for u in range(2):
-                k = side * (KP // 2) + 2 * i + u
-                picked = jnp.dot(tab_t[...], hot_of(k), preferred_element_type=jnp.float32).astype(jnp.bfloat16)
-                seen[k] = picked
-                gw = jnp.dot(picked, cot, preferred_element_type=jnp.float32) * scale
+            first = side * (KP // 2) + i * BATCH
+            hot = jnp.concatenate([hot_of(first + u) for u in range(BATCH)], 1)
+            picked = jnp.dot(tab_t[...], hot, preferred_element_type=jnp.float32).astype(jnp.bfloat16)
+            for u in range(BATCH):
+                k = first + u
+                one = picked[:, u * VOX : (u + 1) * VOX]
+                seen[k] = one
+                gw = jnp.dot(one, cot, preferred_element_type=jnp.float32) * scale
                 for q in range(NF):
                     gw_ref[q, pl.ds(pl.multiple_of(k * IL, IL), IL), :] = gw[q * IL : (q + 1) * IL]
             return 0
 
-        lax.fori_loop(0, KP // 4, step, 0)
+        lax.fori_loop(0, KP // 2 // BATCH, step, 0)
 
     weight_half(other)
     order = (2, 1, 3, 0)
@@ -325,9 +337,12 @@
             jax.ShapeDtypeStruct((ROWS, CO), f32),
             jax.ShapeDtypeStruct((8, HC, CI), f32),
         ),
-        in_specs=[VMEM] * 5,
+        in_specs=[VMEM] + [pl.BlockSpec(memory_space=pl.ANY)] * 4,
         out_specs=(VMEM,) * 4,
         scratch_shapes=[
+            pltpu.VMEM((KP, 1, VOX), jnp.int32),
+            pltpu.VMEM((VOX, CO), bf16),
+            dma(3),
             pltpu.VMEM((8, HC, CI), bf16),
             pltpu.VMEM((NF, 2, KP // 2, IL, CO), bf16),
             pltpu.VMEM((TAB, CI), bf16),

time: 78.3 us -> 76.5 us (0.977)
  Pallas kernels: 71.7 us -> 69.8 us
    pallas_call x1, Pallas kernels: 71.7 us -> 69.8 us  [body(): pl.pallas_call(whole_kernel, out_shape=(jax.ShapeDtypeStruct((VOX, CO), b...]
where the time goes in v5:
time: 76.5 us; the launch traced here: 76.2 us
  Pallas kernels  69.8 us (91%)
  local copies, waits for them, and re-layouts  4.52 us (6%)
  matrix products  1.01 us (1%)
    pallas_call x1, Pallas kernels, body(): pl.pallas_call(whole_kernel, out_shape=(jax.ShapeDtypeStruct((VOX, CO), b...  69.8 us
    unnamed x11, local copies, waits for them, and re-layouts  3.42 us

profile of v5, /device:TPU:1, one launch (start us, length us, event | category | flops | bytes accessed | tf_op | source)
XLA Modules:
  0.0 76.2 jit_solution(262774139777418173)
XLA Ops:
  0.7 0.0 copy-start.3
  0.7 0.0 copy-start.1
  0.7 0.1 stack.35
  0.8 0.6 copy-done.3
  1.4 0.0 copy-start.4
  1.4 0.1 copy-done.1
  1.5 0.5 copy-done.4
  2.0 0.0 copy-start.2
  2.1 0.2 convolution_convert_fusion.b_ref
  2.2 0.6 copy-done.2
  2.8 0.0 copy-start
  2.8 1.0 %copy-done = bf16[64,27,128]{2,0,1:T(8,128)(2,1)S(1)} copy-done((bf16[64,27,128]{2,0,1:T(8,128)(2,1)S(1)}, bf16[64,27,128]{2,0,1:T(8,128)(2,1)}, u32[]{:S(2)}) %copy-start) | copy-done | bytes 442392
  3.8 69.8 %whole.1 = (bf16[128,128]{1,0:T(8,128)(2,1)S(1)}, f32[128,256]{1,0:T(8,128)S(1)}, f32[1792,128]{1,0:T(8,128)S(1)}, f32[8,32,256]{2,1,0:T(8,128)S(1)}) custom-call(bf16[32,256]{1,0:T(8,128)(2,1)S(1)} %convolution_convert_fusion.b_ref, bf16[27,64,128]{2,1,0:T(8,128)(2,1)S(1)} %bitcast.14, bf16[128,256]{1,0:T(8,128)(2,1)S(1)} %copy-done.1, ...), custom_call_target="tpu_custom_call" | custom-call | tf_op jit(solution)/shard_map/whole/pallas_call | solution.py:332
  73.7 0.1 select_reduce_fusion
  73.8 0.8 %fusion = bf16[128,256]{1,0:T(8,128)(2,1)} fusion(f32[128,256]{1,0:T(8,128)S(1)} %get-tuple-element.8, f32[32,256]{1,0:T(8,128)S(1)} %select_reduce_fusion, s32[32]{0:T(128)S(1)} %copy-done.4), kind=kOutput, calls=%fused_computation.1 | convolution fusion | flops 12652544 | bytes 229504 | tf_op jit(solution)/shard_map/dot_general | solution.py:379
  74.6 1.0 %slice.6 = f32[1728,128]{1,0:T(8,128)} slice(f32[1792,128]{1,0:T(8,128)S(1)} %get-tuple-element.10), slice={[0:1728], [0:128]} | slice | bytes 1769472 | tf_op jit(solution)/shard_map/slice | solution.py:380
  75.6 0.6 copy.9
  (3 shorter events, 0.0 us)
Async XLA Ops:
  0.7 0.7 copy-start.3
  0.7 0.8 %copy-start.1 = (bf16[128,256]{1,0:T(8,128)(2,1)S(1)}, bf16[128,256]{1,0:T(8,128)(2,1)}, u32[]{:S(2)}) copy-start(bf16[128,256]{1,0:T(8,128)(2,1)} %feat_in.1) | copy-start | bytes 196612
  1.4 0.7 copy-start.4
  2.0 0.8 copy-start.2
  2.8 1.0 %copy-start = (bf16[64,27,128]{2,0,1:T(8,128)(2,1)S(1)}, bf16[64,27,128]{2,0,1:T(8,128)(2,1)}, u32[]{:S(2)}) copy-start(bf16[64,27,128]{2,0,1:T(8,128)(2,1)} %param.7) | copy-start | bytes 1327108
